TPU v7x, 128 devices: a whole 4x4x4 slice. The times are simulated.
128 devices in a mesh: dp: 4 (over x_hi, core), patch: 32 (over y, x_lo, z).
Axes of the slice: x: 4 (x_hi: 2, x_lo: 2; x = x_hi * 2 + x_lo), y: 4, z: 4, core: 2. Of those that a mesh axis runs over, the one named last changes fastest.
Arguments:
- query_tokens: bfloat16 [4, 64, 128, 768], P('dp', 'patch')
- past_tokens: bfloat16 [4, 256, 128, 768], P('dp', 'patch'), may hold values from -6 to 6
- source_dev: int32 [64, 4, 3], replicated, may hold values from 0 to 31, all different within a row; in each aligned block of 8 rows (0 to 7, 8 to 15, ..., all dimensions but the last counted through in order) at most 2 rows name the same one
- source_slot: int32 [64, 4, 3], replicated, may hold values from 0 to 7
- kept: int32 [64, 4, 3], replicated, may hold values 0 or 1
- w_query: bfloat16 [768, 768], replicated
- w_key: bfloat16 [768, 768], replicated
- w_value: bfloat16 [768, 768], replicated, may hold values from -0.21875 to 0.21875
- w_out: bfloat16 [768, 768], replicated, may hold values from -0.875 to 0.875
- grad_out: bfloat16 [4, 64, 128, 768], P('dp', 'patch'), may hold values from -6 to 6
Outputs:
- attn_out: bfloat16 [4, 64, 128, 768], P('dp', 'patch')
- grad_query_tokens: bfloat16 [4, 64, 128, 768], P('dp', 'patch')
- grad_past_tokens: bfloat16 [4, 256, 128, 768], P('dp', 'patch')
- grad_w_query: float32 [768, 768], replicated
- grad_w_key: float32 [768, 768], replicated
- grad_w_value: float32 [768, 768], replicated
- grad_w_out: float32 [768, 768], replicated
Inputs may be any that keep to these rules, and one draw needn't show every extreme that they name: `source_dev`: row (p, f) lists the devices holding the frame-f blocks that patch p reads: 3 different devices a row. Over the rows of one device's 2 patches, no device is listed more than 2 times, and some device is listed exactly 2 times.
All inputs are finite; a program needn't handle non-finite values.
Results may differ from a plain program's by a relative error of at most 0.013.
The roundings to bfloat16 on the way count: a program that leaves them out, or rounds other values in their place, can miss the bound.
Values may be sent and summed in bfloat16 or wider, within the bound.
A program may use at most 256 MiB of HBM per device.

v0:
```python
import math

import jax
import jax.numpy as jnp
from jax import lax
from jax.sharding import PartitionSpec as P

H = 12
HD = 64


def attend(queries, keys, values, live):
    groups, query_rows, model_width = queries.shape
    key_rows = keys.shape[1]
    inv_scale = 1.0 / math.sqrt(HD)
    head_query = queries.reshape(groups, query_rows, H, HD)
    head_key = keys.reshape(groups, key_rows, H, HD)
    head_value = values.reshape(groups, key_rows, H, HD)
    scores = (
        jnp.einsum("gqhe,gkhe->ghqk", head_query, head_key, preferred_element_type=jnp.float32)
        * inv_scale
    )
    scores = jnp.where(live[:, None, None, :] > 0, scores, -jnp.inf)
    row_max = jnp.max(scores, axis=-1, keepdims=True)
    shifted = jnp.exp(scores - row_max)
    soft_probs = shifted / jnp.sum(shifted, axis=-1, keepdims=True)
    soft_weights = soft_probs.astype(jnp.bfloat16)
    mixed = jnp.einsum(
        "ghqk,gkhe->gqhe", soft_weights, head_value, preferred_element_type=jnp.float32
    )
    mixed = mixed.reshape(groups, query_rows, model_width).astype(jnp.bfloat16)
    return (mixed, soft_probs, soft_weights)


def attend_back(queries, keys, values, soft_probs, soft_weights, upstream):
    groups, query_rows, model_width = queries.shape
    key_rows = keys.shape[1]
    inv_scale = 1.0 / math.sqrt(HD)
    head_query = queries.reshape(groups, query_rows, H, HD)
    head_key = keys.reshape(groups, key_rows, H, HD)
    head_value = values.reshape(groups, key_rows, H, HD)
    head_up = upstream.reshape(groups, query_rows, H, HD)
    grad_prob = jnp.einsum(
        "gqhe,gkhe->ghqk", head_up, head_value, preferred_element_type=jnp.float32
    )
    row_delta = jnp.sum(soft_probs * grad_prob, axis=-1, keepdims=True)
    grad_score = (soft_probs * (grad_prob - row_delta) * inv_scale).astype(jnp.bfloat16)
    grad_q = jnp.einsum("ghqk,gkhe->gqhe", grad_score, head_key, preferred_element_type=jnp.float32)
    grad_k = jnp.einsum(
        "ghqk,gqhe->gkhe", grad_score, head_query, preferred_element_type=jnp.float32
    )
    grad_v = jnp.einsum(
        "ghqk,gqhe->gkhe", soft_weights, head_up, preferred_element_type=jnp.float32
    )
    grad_q = grad_q.reshape(groups, query_rows, model_width).astype(jnp.bfloat16)
    grad_k = grad_k.reshape(groups, key_rows, model_width).astype(jnp.bfloat16)
    grad_v = grad_v.reshape(groups, key_rows, model_width).astype(jnp.bfloat16)
    return (grad_q, grad_k, grad_v)


def forward_group(inputs):
    queries, keys, values, live = inputs
    mixed, soft_probs, soft_weights = attend(queries[None], keys[None], values[None], live[None])
    return (mixed[0], soft_probs[0], soft_weights[0])


def backward_group(inputs):
    queries, keys, values, soft_probs, soft_weights, upstream = inputs
    grad_q, grad_k, grad_v = attend_back(
        queries[None],
        keys[None],
        values[None],
        soft_probs[None],
        soft_weights[None],
        upstream[None],
    )
    return (grad_q[0], grad_k[0], grad_v[0])


def transpose_dot(left, right):
    return jnp.einsum("nd,ed->ne", left, right, preferred_element_type=jnp.float32)


def outer_sum(left, right):
    return jnp.einsum("nd,ne->de", left, right, preferred_element_type=jnp.float32)


def body(
    query_tokens,
    past_tokens,
    source_dev,
    source_slot,
    kept,
    w_query,
    w_key,
    w_value,
    w_out,
    grad_out,
):
    batch_local, patch_local, block_rows, model_width = query_tokens.shape
    slots_local = past_tokens.shape[1]
    peer_count = lax.axis_size("patch")
    device = lax.axis_index("patch")
    requests = source_dev.shape[1] * source_dev.shape[2]
    per_device = patch_local * requests
    capacity = max(2, (per_device + peer_count - 1) // peer_count + 1)
    owners = source_dev.reshape(peer_count, per_device)
    places = source_slot.reshape(peer_count, per_device)
    live_all = kept.reshape(peer_count, per_device)
    request_order = jnp.arange(per_device)
    earlier = request_order[:, None] > request_order[None, :]
    matches = (owners[:, :, None] == owners[:, None, :]) & earlier[None]
    slot_rank = jnp.sum(matches.astype(jnp.int32), axis=2)
    from_here = (owners == device) & (live_all > 0)
    slot_hit = (slot_rank[:, :, None] == jnp.arange(capacity)[None, None, :]) & from_here[
        :, :, None
    ]
    place_hit = places[:, :, None] == jnp.arange(slots_local)[None, None, :]
    chooser = jnp.einsum(
        "dqc,dqs->dcs", slot_hit.astype(jnp.float32), place_hit.astype(jnp.float32)
    ).astype(jnp.bfloat16)
    outgoing = jnp.einsum(
        "dcs,bsnw->bdcnw", chooser, past_tokens, preferred_element_type=jnp.float32
    ).astype(jnp.bfloat16)
    incoming = lax.all_to_all(outgoing, "patch", split_axis=1, concat_axis=1, tiled=True)
    my_owner = lax.dynamic_index_in_dim(owners, device, 0, keepdims=False)
    my_rank = lax.dynamic_index_in_dim(slot_rank, device, 0, keepdims=False)
    my_live = lax.dynamic_index_in_dim(live_all, device, 0, keepdims=False)
    position = my_owner * capacity + my_rank
    arrived = incoming.reshape(batch_local, peer_count * capacity, block_rows, model_width)
    fetched = jnp.take(arrived, position, axis=1)
    fetched_rows = fetched.reshape(batch_local * per_device * block_rows, model_width)
    w_proj = jnp.concatenate([w_query, w_key, w_value], axis=1)
    w_pair = jnp.concatenate([w_key, w_value], axis=1)
    token_rows = query_tokens.reshape(-1, model_width)
    own_proj = jnp.dot(token_rows, w_proj, preferred_element_type=jnp.float32).astype(jnp.bfloat16)
    far_proj = jnp.dot(fetched_rows, w_pair, preferred_element_type=jnp.float32).astype(
        jnp.bfloat16
    )
    groups = batch_local * patch_local
    far_rows = requests * block_rows
    queries = own_proj[:, :model_width].reshape(groups, block_rows, model_width)
    all_keys = jnp.concatenate(
        [
            own_proj[:, model_width : 2 * model_width].reshape(groups, block_rows, model_width),
            far_proj[:, :model_width].reshape(groups, far_rows, model_width),
        ],
        axis=1,
    )
    all_values = jnp.concatenate(
        [
            own_proj[:, 2 * model_width :].reshape(groups, block_rows, model_width),
            far_proj[:, model_width:].reshape(groups, far_rows, model_width),
        ],
        axis=1,
    )
    live_far = jnp.repeat(my_live.reshape(patch_local, requests), block_rows, axis=1)
    live_row = jnp.concatenate([jnp.ones((patch_local, block_rows), jnp.int32), live_far], axis=1)
    live_row = jnp.tile(live_row, (batch_local, 1))
    mixed, soft_probs, soft_weights = lax.map(
        forward_group, (queries, all_keys, all_values, live_row)
    )
    mixed_rows = mixed.reshape(-1, model_width)
    result = jnp.dot(mixed_rows, w_out, preferred_element_type=jnp.float32).astype(jnp.bfloat16)
    grad_rows = grad_out.reshape(-1, model_width)
    upstream = transpose_dot(grad_rows, w_out).astype(jnp.bfloat16)
    grad_wo = outer_sum(mixed_rows, grad_rows)
    grad_q, grad_k, grad_v = lax.map(
        backward_group,
        (
            queries,
            all_keys,
            all_values,
            soft_probs,
            soft_weights,
            upstream.reshape(groups, block_rows, model_width),
        ),
    )
    q_rows = grad_q.reshape(-1, model_width)
    own_k = grad_k[:, :block_rows].reshape(-1, model_width)
    own_v = grad_v[:, :block_rows].reshape(-1, model_width)
    far_k = grad_k[:, block_rows:].reshape(-1, model_width)
    far_v = grad_v[:, block_rows:].reshape(-1, model_width)
    grad_tokens = (
        transpose_dot(q_rows, w_query) + transpose_dot(own_k, w_key) + transpose_dot(own_v, w_value)
    ).astype(jnp.bfloat16)
    far_grad = (transpose_dot(far_k, w_key) + transpose_dot(far_v, w_value)).astype(jnp.bfloat16)
    far_grad = far_grad.reshape(batch_local, per_device, block_rows, model_width)
    back_rows = jnp.zeros(
        (batch_local, peer_count * capacity, block_rows, model_width), jnp.bfloat16
    )
    back_rows = back_rows.at[:, position].set(far_grad)
    returned = lax.all_to_all(
        back_rows.reshape(batch_local, peer_count, capacity, block_rows, model_width),
        "patch",
        split_axis=1,
        concat_axis=1,
        tiled=True,
    )
    past_grad = jnp.einsum(
        "dcs,bdcnw->bsnw", chooser, returned, preferred_element_type=jnp.float32
    ).astype(jnp.bfloat16)
    grad_wq = outer_sum(token_rows, q_rows)
    grad_wk = outer_sum(token_rows, own_k) + outer_sum(fetched_rows, far_k)
    grad_wv = outer_sum(token_rows, own_v) + outer_sum(fetched_rows, far_v)
    grad_wq, grad_wk, grad_wv, grad_wo = lax.psum(
        (grad_wq, grad_wk, grad_wv, grad_wo), ("dp", "patch")
    )
    inv_total = 1.0 / math.sqrt(
        lax.axis_size("dp") * batch_local * peer_count * patch_local * block_rows
    )
    return (
        result.reshape(query_tokens.shape),
        grad_tokens.reshape(query_tokens.shape),
        past_grad,
        grad_wq * inv_total,
        grad_wk * inv_total,
        grad_wv * inv_total,
        grad_wo * inv_total,
    )


def solution(mesh):
    placed = (
        P("dp", "patch", None, None),
        P("dp", "patch", None, None),
        P(),
        P(),
        P(),
        P(),
        P(),
        P(),
        P(),
        P("dp", "patch", None, None),
    )
    return jax.shard_map(
        body,
        mesh=mesh,
        in_specs=placed,
        out_specs=(
            P("dp", "patch", None, None),
            P("dp", "patch", None, None),
            P("dp", "patch", None, None),
            P(),
            P(),
            P(),
            P(),
        ),
        check_vma=False,
    )
```

profile of v0, /device:TPU:1, one launch (start us, length us, event | category | flops | bytes accessed | tf_op | source)
XLA Modules:
  0.0 947.5 jit_solution(16771115224350771100)
XLA Ops:
  15.9 21.9 %copy.171 = bf16[1,32,2,128,768]{4,3,2,0,1:T(8,128)(2,1)} copy(bf16[1,32,2,128,768]{4,1,3,2,0:T(8,128)(2,1)S(1)} %convert_bitcast_fusion) | data formatting | bytes 25165824 | tf_op jit(solution)/shard_map/convert_element_type | solution.py:124
  37.8 10.3 %all-to-all-start = ((bf16[1,32,2,128,768]{4,3,2,0,1:T(8,128)(2,1)}), bf16[1,32,2,128,768]{4,3,2,0,1:T(8,128)(2,1)}, u32[]{:S(2)}, u32[]{:S(2)}) async-start(bf16[1,32,2,128,768]{4,3,2,0,1:T(8,128)(2,1)} %copy.171), calls=%async_computation | async-start | bytes 25165824 | tf_op jit(solution)/shard_map/all_to_all | solution.py:125
  55.1 223.6 %all-to-all-done = bf16[1,32,2,128,768]{4,3,2,0,1:T(8,128)(2,1)} async-done(((bf16[1,32,2,128,768]{4,3,2,0,1:T(8,128)(2,1)}), bf16[1,32,2,128,768]{4,3,2,0,1:T(8,128)(2,1)}, u32[]{:S(2)}, u32[]{:S(2)}) %all-to-all-start) | async-done | bytes 12582944 | tf_op jit(solution)/shard_map/all_to_all | solution.py:125
  278.6 7.7 gather_fusion
  289.7 9.9 %convolution_convert_fusion.3 = bf16[3072,1536]{1,0:T(8,128)(2,1)} fusion(bf16[3072,768]{1,0:T(8,128)(2,1)S(1)} %bitcast_select_fusion.1, bf16[768,768]{1,0:T(8,128)(2,1)S(1)} %copy-done.16, bf16[768,768]{1,0:T(8,128)(2,1)S(1)} %copy-done.13), kind=kOutput, calls=%fused_computation.46 | convolution fusion | flops 7257194496 | bytes 16515072 | tf_op jit(solution)/shard_map/dot_general | solution.py:137
  299.6 7.9 fusion.56
  307.5 6.7 copy.173
  314.2 6.8 copy.175
  321.0 8.5 pad_maximum_fusion
  329.6 73.8 %while.28 = (s32[]{:T(128)}, bf16[2,128,768]{2,1,0:T(8,128)(2,1)S(1)}, f32[2,12,128,1664]{3,2,1,0:T(8,128)}, bf16[2,12,128,1664]{3,2,1,0:T(8,128)(2,1)}, bf16[2,...) while((s32[]{:T(128)}, ...), condition=%wide.region_4.5_spmd, body=%wide.region_1.0_spmd.sunk | while | flops 672304384 | bytes 83390360 | solution.py:160
  330.1 5.1 constant_dynamic-slice_fusion.14
  335.3 8.5 fusion.124
  343.8 9.6 %bitcast_dynamic-update-slice_fusion.4 = (bf16[2,12,128,1664]{3,2,1,0:T(8,128)(2,1)}, bf16[12,128,1664]{2,1,0:T(8,128)(2,1)}) fusion(bf16[2,12,128,1664]{3,2,1,0:T(8,128)(2,1)} %get-tuple-element.460, s32[]{:T(128)S(6)} %copy.244, f32[12,128,1664]{2,1,0:T(8,128)} %get-tuple-element.430, f32[12,128]{1,0:T(8,128)S(1)} %get-tuple-element.431), kind=kLoop, calls=%fused_computation.27.clone.1 | loop fusion | flops 5111808 | bytes 20453380 | tf_op jit(solution)/shard_map/while/body/jit(dynamic_update_index_in_dim)/dynamic_update_slice | solution.py:160
  358.0 8.8 bitcast_dynamic-update-slice_fusion.5
  366.8 5.1 constant_dynamic-slice_fusion.14
  372.0 8.5 fusion.124
  380.5 9.6 %bitcast_dynamic-update-slice_fusion.4 = (bf16[2,12,128,1664]{3,2,1,0:T(8,128)(2,1)}, bf16[12,128,1664]{2,1,0:T(8,128)(2,1)}) fusion(bf16[2,12,128,1664]{3,2,1,0:T(8,128)(2,1)} %get-tuple-element.460, s32[]{:T(128)S(6)} %copy.244, f32[12,128,1664]{2,1,0:T(8,128)} %get-tuple-element.430, f32[12,128]{1,0:T(8,128)S(1)} %get-tuple-element.431), kind=kLoop, calls=%fused_computation.27.clone.1 | loop fusion | flops 5111808 | bytes 20453380 | tf_op jit(solution)/shard_map/while/body/jit(dynamic_update_index_in_dim)/dynamic_update_slice | solution.py:160
  394.7 8.7 bitcast_dynamic-update-slice_fusion.5
  404.1 108.9 %while.29 = (s32[]{:T(128)}, bf16[2,128,768]{2,1,0:T(8,128)(2,1)S(1)}, bf16[2,1664,768]{2,1,0:T(8,128)(2,1)}, bf16[2,1664,768]{2,1,0:T(8,128)(2,1)}, bf16[2,1664...) while((s32[]{:T(128)}, ...), condition=%wide.region_7.8_spmd, body=%wide.region_5.7_spmd.sunk | while | flops 1326610944 | bytes 105001104 | solution.py:168
  409.8 9.4 fusion.133
  419.2 10.3 %fusion.134 = bf16[12,128,1664]{2,1,0:T(8,128)(2,1)} fusion(f32[12,128,1664]{2,1,0:T(8,128)} %get-tuple-element.444, f32[2,12,128,1664]{3,2,1,0:T(8,128)} %get-tuple-element.502, s32[]{:T(128)S(6)} %copy.256, f32[12,128]{1,0:T(8,128)S(1)} %get-tuple-element.445), kind=kLoop, calls=%fused_computation.7.clone.1 | loop fusion | flops 10223616 | bytes 25565188 | tf_op jit(solution)/shard_map/reshape.27
  429.5 5.2 convolution_convert_fusion.11
  464.2 9.4 fusion.133
  473.6 10.3 %fusion.134 = bf16[12,128,1664]{2,1,0:T(8,128)(2,1)} fusion(f32[12,128,1664]{2,1,0:T(8,128)} %get-tuple-element.444, f32[2,12,128,1664]{3,2,1,0:T(8,128)} %get-tuple-element.502, s32[]{:T(128)S(6)} %copy.256, f32[12,128]{1,0:T(8,128)S(1)} %get-tuple-element.445), kind=kLoop, calls=%fused_computation.7.clone.1 | loop fusion | flops 10223616 | bytes 25565188 | tf_op jit(solution)/shard_map/reshape.27
  483.9 5.2 convolution_convert_fusion.11
  521.1 5.8 add_convert_fusion
  527.0 6.0 broadcast.176
  533.0 15.3 %scatter_fusion = bf16[64,128,768]{2,1,0:T(8,128)(2,1)} fusion(bf16[64,128,768]{2,1,0:T(8,128)(2,1)} %broadcast.176, s32[24]{0:T(128)S(1)} %copy-done.24, bf16[24,128,768]{2,1,0:T(8,128)(2,1)} %bitcast.251), kind=kCustom, calls=%fused_computation.1 | custom fusion | bytes 14155872 | tf_op jit(solution)/shard_map/scatter | solution.py:192
  548.3 23.6 %copy.185 = bf16[1,32,2,128,768]{4,2,3,0,1:T(2,128)(2,1)} copy(bf16[1,32,2,128,768]{4,3,2,1,0:T(8,128)(2,1)} %bitcast.228) | data formatting | bytes 25165824 | tf_op jit(solution)/shard_map/reshape | solution.py:194
  571.9 5.3 all-to-all-start.1
  603.9 308.2 %all-reduce.4.cloned.1.call-done = (f32[768,768]{0,1:T(8,128)}, f32[768,768]{0,1:T(8,128)}, f32[768,768]{0,1:T(8,128)}, f32[768,768]{0,1:T(8,128)}) async-done(((f32[768,768]{0,1:T(8,128)}, f32[768,768]{0,1:T(8,128)}, f32[768,768]{0,1:T(8,128)}, f32[768,768]{0,1:T(8,128)}), (f32[768,768]{0,1:T(8,128)}, f32[768,768]{0,1:T(8,128)}, f32[768,768]{0,1:T(8,128)}, ...) | async-done | bytes 9437200 | tf_op jit(solution)/shard_map/psum | solution.py:206
  927.7 11.3 %fusion.37 = bf16[1,8,128,768]{3,1,2,0:T(8,128)(2,1)S(1)} fusion(bf16[1,32,2,128,768]{4,2,3,0,1:T(2,128)(2,1)} %all-to-all-done.1, bf16[32,2,8]{0,2,1:T(8,128)(2,1)S(1)} %copy-done.20), kind=kOutput, calls=%fused_computation.68 | convolution fusion | flops 101449728 | bytes 14156800 | tf_op jit(solution)/shard_map/dcs,bdcnw->bsnw/dot_general | solution.py:200
  (166 shorter events, 139.4 us)
Async XLA Ops:
  7.2 47.4 %copy-start = (bf16[768,768]{1,0:T(8,128)(2,1)S(1)}, bf16[768,768]{1,0:T(8,128)(2,1)}, u32[]{:S(2)}) copy-start(bf16[768,768]{1,0:T(8,128)(2,1)} %param.22) | copy-start | bytes 3538948
  10.7 5.1 copy-start.19
  37.7 10.4 %copy-start.6 = (bf16[1,2,128,768]{3,2,1,0:T(8,128)(2,1)S(1)}, bf16[1,2,128,768]{3,2,1,0:T(8,128)(2,1)}, u32[]{:S(2)}) copy-start(bf16[1,2,128,768]{3,2,1,0:T(8,128)(2,1)} %param.14) | copy-start | bytes 1179652
  37.8 10.4 %copy-start.12 = (bf16[768,768]{1,0:T(8,128)(2,1)S(1)}, bf16[768,768]{1,0:T(8,128)(2,1)}, u32[]{:S(2)}) copy-start(bf16[768,768]{1,0:T(8,128)(2,1)} %param.20) | copy-start | bytes 3538948
  37.8 240.9 %all-to-all-start = ((bf16[1,32,2,128,768]{4,3,2,0,1:T(8,128)(2,1)}), bf16[1,32,2,128,768]{4,3,2,0,1:T(8,128)(2,1)}, u32[]{:S(2)}, u32[]{:S(2)}) async-start(bf16[1,32,2,128,768]{4,3,2,0,1:T(8,128)(2,1)} %copy.171), calls=%async_computation | async-start | bytes 25165824 | tf_op jit(solution)/shard_map/all_to_all | solution.py:125
  50.9 3.6 copy-start.8
  286.3 3.4 copy-start.13
  286.3 3.4 copy-start.16
  314.2 6.8 copy-start.10
  314.2 6.8 copy-start.11
  343.8 9.6 %copy-start.1 = (bf16[1,1664,768]{1,2,0:T(8,128)(2,1)S(1)}, bf16[1,1664,768]{1,2,0:T(8,128)(2,1)}, u32[]{:S(2)}) copy-start(bf16[1,1664,768]{1,2,0:T(8,128)(2,1)} %get-tuple-element.428) | copy-start | bytes 7667716 | tf_op jit(solution)/shard_map/while
  380.5 9.6 %copy-start.1 = (bf16[1,1664,768]{1,2,0:T(8,128)(2,1)S(1)}, bf16[1,1664,768]{1,2,0:T(8,128)(2,1)}, u32[]{:S(2)}) copy-start(bf16[1,1664,768]{1,2,0:T(8,128)(2,1)} %get-tuple-element.428) | copy-start | bytes 7667716 | tf_op jit(solution)/shard_map/while
  513.1 2.8 copy-start.14
  513.1 6.7 slice-start
  515.9 3.9 copy-start.3
  515.9 3.9 slice-start.1
  519.8 1.3 copy-start.17
  520.1 6.8 copy-start.2
  527.0 6.1 copy-start.24
  571.9 7.9 copy-start.7
  571.9 355.7 %all-to-all-start.1 = ((bf16[1,32,2,128,768]{4,2,3,0,1:T(2,128)(2,1)}), bf16[1,32,2,128,768]{4,2,3,0,1:T(2,128)(2,1)}, u32[]{:S(2)}, u32[]{:S(2)}) async-start(bf16[1,32,2,128,768]{4,2,3,0,1:T(2,128)(2,1)} %copy.185), calls=%async_computation.1 | async-start | bytes 25165824 | tf_op jit(solution)/shard_map/all_to_all | solution.py:193
  577.2 4.5 copy-start.5
  577.2 6.5 copy-start.22
  577.2 335.0 %all-reduce.4.cloned.1.call-start = ((), (), s32[]{:S(2)}) async-start(), calls=%async_computation.2 | async-start | bytes 18874368 | tf_op jit(solution)/shard_map/psum | solution.py:206
  577.6 4.1 copy-start.9
  581.7 5.0 slice-start.4
  583.6 3.1 slice-start.5
  583.6 9.3 slice-start.2
  586.7 6.2 slice-start.3
  599.1 3.0 copy-start.15
  599.1 3.5 copy-start.18
  923.8 3.8 copy-start.20
  (3 other events, 1.8 us)
Sparse Core Ops, SparseCore 0:
  599.2 312.8 all-reduce.3
where the time goes:
time: 955 us; the launch traced here: 947 us
  waiting for transfers between devices  532 us (56%)
  local copies, waits for them, and re-layouts  169 us (18%)
  matrix products  135 us (14%)
  other arithmetic  80.4 us (8%)
  starting transfers between devices  16.1 us (2%)
  between operations  14.7 us (2%)
    psum x1, waiting for transfers between devices, body(): lax.psum((grad_wq, grad_wk, grad_wv, grad_wo), ('dp', 'patch'))  308 us
    all_to_all x1, waiting for transfers between devices, body(): lax.all_to_all(outgoing, 'patch', split_axis=1, concat_axis=1, tiled=True)  224 us
    dynamic_update_slice x4, other arithmetic, body(): lax.map(forward_group, (queries, all_keys, all_values, live_row))  36.7 us
    dynamic_update_slice x6, local copies, waits for them, and re-layouts, body(): lax.map(backward_group, (queries, all_keys, all_values, soft_probs, soft_...  28.3 us
    reshape x1, local copies, waits for them, and re-layouts, body(): back_rows.reshape(batch_local, peer_count, capacity, block_rows, model_wi...  23.6 us
    convert_element_type x1, local copies, waits for them, and re-layouts, body(): outgoing = jnp.einsum('dcs,bsnw->bdcnw', chooser, past_tokens, preferred_...  21.9 us
    dynamic_slice x14, local copies, waits for them, and re-layouts, body(): lax.map(forward_group, (queries, all_keys, all_values, live_row))  21.3 us
    another operation x4, other arithmetic  20.6 us
  transfers between devices with their start and end apart: 3, of which 2 were waited for; matrix products, arithmetic and copies ran while one was open for 5% of the time, Pallas kernels for 0%

commit v1 on v0

v1 whole, which is shorter than its diff:
```python
import math

import jax
import jax.numpy as jnp
from jax import lax
from jax.experimental import pallas as pl
from jax.experimental.pallas import tpu as pltpu
from jax.sharding import PartitionSpec as P

H = 12
HD = 64
F32 = jnp.float32
BF16 = jnp.bfloat16
NN = (((1,), (0,)), ((), ()))
NT = (((1,), (1,)), ((), ()))
TN = (((0,), (0,)), ((), ()))


def mm(a, b, dims=NN):
    return lax.dot_general(a, b, dims, preferred_element_type=F32)


def gather_blocks(source, index):
    count = index.shape[0]

    def kernel(index_ref, source_ref, out_ref, sems):
        def copy(i):
            return pltpu.make_async_copy(
                source_ref.at[index_ref[i]], out_ref.at[i], sems.at[i]
            )

        @pl.loop(0, count)
        def _(i):
            copy(i).start()

        @pl.loop(0, count)
        def _(i):
            copy(i).wait()

    return pl.pallas_call(
        kernel,
        out_shape=jax.ShapeDtypeStruct((count,) + source.shape[1:], source.dtype),
        grid_spec=pltpu.PrefetchScalarGridSpec(
            num_scalar_prefetch=1,
            grid=(),
            in_specs=[pl.BlockSpec(memory_space=pl.ANY)],
            out_specs=pl.BlockSpec(memory_space=pl.ANY),
            scratch_shapes=[pltpu.SemaphoreType.DMA((count,))],
        ),
        name="gather_blocks",
    )(index, source)


def scatter_sum(source, target, used, outputs):
    count, rows, width = source.shape
    step = 8

    def kernel(target_ref, used_ref, source_ref, out_ref, acc):
        t = pl.program_id(0)

        @pl.when(t == 0)
        def _():
            acc[...] = jnp.zeros_like(acc)

        for j in range(step):
            @pl.when(used_ref[t * step + j] > 0)
            def _():
                m = target_ref[t * step + j]
                acc[m] = acc[m] + source_ref[j].astype(F32)

        @pl.when(t == pl.num_programs(0) - 1)
        def _():
            out_ref[...] = acc[...].astype(out_ref.dtype)

    return pl.pallas_call(
        kernel,
        out_shape=jax.ShapeDtypeStruct((outputs, rows, width), source.dtype),
        grid_spec=pltpu.PrefetchScalarGridSpec(
            num_scalar_prefetch=2,
            grid=(count // step,),
            in_specs=[pl.BlockSpec((step, rows, width), lambda t, *_: (t, 0, 0))],
            out_specs=pl.BlockSpec((outputs, rows, width), lambda t, *_: (0, 0, 0)),
            scratch_shapes=[pltpu.VMEM((outputs, rows, width), F32)],
        ),
        compiler_params=pltpu.CompilerParams(vmem_limit_bytes=48 << 20),
        name="scatter_sum",
    )(target, used, source)


def layer(position, live, arrived, tokens, grad_out, w_query, w_pair, w_out, slots):
    patches, block, width = tokens.shape
    requests = position.shape[0] // patches
    far = requests * block
    rows = block + far
    chunks = 4
    chunk = far // chunks
    pairs = width // 128
    parts = requests + 1

    def kernel(
        position_ref, live_ref, arrived_ref, tokens_ref, grad_ref, wq_ref, wkv_ref, wo_ref,
        attn_ref, tokgrad_ref, fargrad_ref, x_ref, dkv_ref, dq_ref, mixed_ref,
        key_s, val_s, q_s, up_s, s_s, dp_s, pb_s, ds_s, fg_s, in_sem, out_sem,
    ):
        p = pl.program_id(0)

        def fetch(r):
            return pltpu.make_async_copy(
                arrived_ref.at[position_ref[p * requests + r]],
                x_ref.at[0, pl.ds(block + r * block, block)],
                in_sem.at[r],
            )

        for r in range(requests):
            fetch(r).start()
        tok = tokens_ref[0]
        x_ref[0, 0:block] = tok
        q_s[...] = mm(tok, wq_ref[...]).astype(BF16)
        own = mm(tok, wkv_ref[...]).astype(BF16)
        key_s[0:block] = own[:, :width]
        val_s[0:block] = own[:, width:]
        up_s[...] = mm(grad_ref[0], wo_ref[...], NT).astype(BF16)
        for r in range(requests):
            fetch(r).wait()

        @pl.loop(0, chunks)
        def _(c):
            at = pl.multiple_of(block + c * chunk, 128)
            x = x_ref[0, pl.ds(at, chunk)]
            key_s[pl.ds(at, chunk)] = mm(x, wkv_ref[:, :width]).astype(BF16)
            val_s[pl.ds(at, chunk)] = mm(x, wkv_ref[:, width:]).astype(BF16)

        low = lax.broadcasted_iota(jnp.int32, (block, 128), 1) < HD
        zero = jnp.zeros((block, 128), BF16)

        @pl.loop(0, pairs)
        def _(j):
            lanes = pl.ds(pl.multiple_of(j * 128, 128), 128)
            k = key_s[:, lanes]
            v = val_s[:, lanes]
            q = q_s[:, lanes] * jnp.asarray(1.0 / math.sqrt(HD), BF16)
            u = up_s[:, lanes]
            q2 = jnp.concatenate([jnp.where(low, q, zero), jnp.where(low, zero, q)], axis=0)
            u2 = jnp.concatenate([jnp.where(low, u, zero), jnp.where(low, zero, u)], axis=0)
            s_s[...] = mm(k, q2, NT)
            dp_s[...] = mm(v, u2, NT)

            def bias(r):
                dead = live_ref[p * requests + jnp.maximum(r - 1, 0)] == 0
                return jnp.where((r > 0) & dead, -jnp.inf, 0.0).astype(F32)

            def part(r):
                return pl.ds(pl.multiple_of(r * block, block), block)

            def largest(r, m):
                s = s_s[part(r)] + bias(r)
                return jnp.maximum(m, jnp.max(s.reshape(block // 8, 8, 2 * block), axis=0))

            m = lax.fori_loop(0, parts, largest, jnp.full((8, 2 * block), -jnp.inf, F32))
            m = jnp.max(m, axis=0, keepdims=True)

            def exps(r, carry):
                total, delta = carry
                e = jnp.exp(s_s[part(r)] + bias(r) - m)
                s_s[part(r)] = e
                g = e * dp_s[part(r)]
                fold = lambda t: jnp.sum(t.reshape(block // 8, 8, 2 * block), axis=0)
                return total + fold(e), delta + fold(g)

            nil = jnp.zeros((8, 2 * block), F32)
            total, delta = lax.fori_loop(0, parts, exps, (nil, nil))
            inverse = 1.0 / jnp.sum(total, axis=0, keepdims=True)
            delta = jnp.sum(delta, axis=0, keepdims=True) * inverse

            @pl.loop(0, parts)
            def _(r):
                prob = s_s[part(r)] * inverse
                pb_s[part(r)] = prob.astype(BF16)
                ds_s[part(r)] = (prob * (dp_s[part(r)] - delta)).astype(BF16)

            pb = pb_s[...]
            ds = ds_s[...]
            dkv_ref[0, :, lanes] = mm(ds, q2).astype(BF16)
            dkv_ref[0, :, pl.ds(pl.multiple_of(width + j * 128, 128), 128)] = mm(pb, u2).astype(BF16)
            o = mm(pb, v, TN)
            mixed_ref[0, :, lanes] = jnp.where(low, o[:block], o[block:]).astype(BF16)
            dq = mm(ds, k, TN)
            dq = jnp.where(low, dq[:block], dq[block:]) * (1.0 / math.sqrt(HD))
            dq_ref[0, :, lanes] = dq.astype(BF16)

        attn_ref[0] = mm(mixed_ref[0], wo_ref[...]).astype(BF16)
        tokgrad_ref[0] = (
            mm(dq_ref[0], wq_ref[...], NT) + mm(dkv_ref[0, 0:block], wkv_ref[...], NT)
        ).astype(BF16)

        @pl.loop(0, chunks)
        def _(c):
            at = pl.multiple_of(block + c * chunk, 128)
            g = mm(dkv_ref[0, pl.ds(at, chunk)], wkv_ref[...], NT).astype(BF16)
            fg_s[pl.ds(pl.multiple_of(c * chunk, 128), chunk)] = g

        def put(r):
            return pltpu.make_async_copy(
                fg_s.at[pl.ds(r * block, block)],
                fargrad_ref.at[position_ref[p * requests + r]],
                out_sem.at[r],
            )

        for r in range(requests):
            put(r).start()
        for r in range(requests):
            put(r).wait()

    per_patch = lambda n, w: pl.BlockSpec((1, n, w), lambda p, *_: (p, 0, 0))
    whole = lambda a: pl.BlockSpec(a.shape, lambda p, *_: (0, 0), pipeline_mode=pl.Buffered(1))
    hbm = pl.BlockSpec(memory_space=pl.ANY)
    shape = lambda *s: jax.ShapeDtypeStruct(s, BF16)
    return pl.pallas_call(
        kernel,
        out_shape=(
            shape(patches, block, width),
            shape(patches, block, width),
            shape(slots, block, width),
            shape(patches, rows, width),
            shape(patches, rows, 2 * width),
            shape(patches, block, width),
            shape(patches, block, width),
        ),
        grid_spec=pltpu.PrefetchScalarGridSpec(
            num_scalar_prefetch=2,
            grid=(patches,),
            in_specs=[
                hbm, per_patch(block, width), per_patch(block, width),
                whole(w_query), whole(w_pair), whole(w_out),
            ],
            out_specs=(
                per_patch(block, width), per_patch(block, width), hbm, per_patch(rows, width),
                per_patch(rows, 2 * width), per_patch(block, width), per_patch(block, width),
            ),
            scratch_shapes=[
                pltpu.VMEM((rows, width), BF16),
                pltpu.VMEM((rows, width), BF16),
                pltpu.VMEM((block, width), BF16),
                pltpu.VMEM((block, width), BF16),
                pltpu.VMEM((rows, 2 * block), F32),
                pltpu.VMEM((rows, 2 * block), F32),
                pltpu.VMEM((rows, 2 * block), BF16),
                pltpu.VMEM((rows, 2 * block), BF16),
                pltpu.VMEM((far, width), BF16),
                pltpu.SemaphoreType.DMA((requests,)),
                pltpu.SemaphoreType.DMA((requests,)),
            ],
        ),
        compiler_params=pltpu.CompilerParams(vmem_limit_bytes=60 << 20),
        name="layer",
    )(position, live, arrived, tokens, grad_out, w_query, w_pair, w_out)


def outer_sum(left, right):
    return lax.dot_general(left, right, TN, preferred_element_type=F32)


def body(
    query_tokens, past_tokens, source_dev, source_slot, kept, w_query, w_key, w_value, w_out,
    grad_out,
):
    _, patches, block, width = query_tokens.shape
    tokens, grads, past = query_tokens[0], grad_out[0], past_tokens[0]
    peers = lax.axis_size("patch")
    device = lax.axis_index("patch")
    per_device = patches * source_dev.shape[1] * source_dev.shape[2]
    cap = 2
    owners = source_dev.reshape(peers, per_device)
    places = source_slot.reshape(peers, per_device)
    order = jnp.arange(per_device)
    matches = (owners[:, :, None] == owners[:, None, :]) & (order[:, None] > order[None, :])
    rank = jnp.sum(matches.astype(jnp.int32), axis=2)
    hit = (rank[:, :, None] == jnp.arange(cap)) & (owners == device)[:, :, None]
    out_place = jnp.sum(jnp.where(hit, places[:, :, None], 0), axis=1).reshape(-1)
    out_used = jnp.sum(hit.astype(jnp.int32), axis=1).reshape(-1)
    mine = owners[device] * cap + rank[device]
    live = kept.reshape(peers, per_device)[device]

    outgoing = gather_blocks(past, out_place)
    arrived = lax.all_to_all(outgoing, "patch", split_axis=0, concat_axis=0, tiled=True)
    w_pair = jnp.concatenate([w_key, w_value], axis=1)
    attn, token_grad, far_grad, x, dkv, dq, mixed = layer(
        mine, live, arrived, tokens, grads, w_query, w_pair, w_out, peers * cap
    )
    returned = lax.all_to_all(far_grad, "patch", split_axis=0, concat_axis=0, tiled=True)
    past_grad = scatter_sum(returned, out_place, out_used, past.shape[0])
    flat = lambda a: a.reshape(-1, a.shape[-1])
    grad_pair = outer_sum(flat(x), flat(dkv))
    grad_wq = outer_sum(flat(tokens), flat(dq))
    grad_wo = outer_sum(flat(mixed), flat(grads))
    grad_pair, grad_wq, grad_wo = lax.psum((grad_pair, grad_wq, grad_wo), ("dp", "patch"))
    scale = 1.0 / math.sqrt(lax.axis_size("dp") * peers * patches * block)
    return (
        attn[None],
        token_grad[None],
        past_grad[None],
        grad_wq * scale,
        grad_pair[:, :width] * scale,
        grad_pair[:, width:] * scale,
        grad_wo * scale,
    )


def solution(mesh):
    split = P("dp", "patch", None, None)
    return jax.shard_map(
        body,
        mesh=mesh,
        in_specs=(split, split, P(), P(), P(), P(), P(), P(), P(), split),
        out_specs=(split, split, split, P(), P(), P(), P()),
        check_vma=False,
    )
```

time: 955 us -> 1080 us (1.13)
  Pallas kernels: 0 us -> 463 us
  local copies, waits for them, and re-layouts: 169 us -> 13.9 us
  matrix products: 135 us -> 16.1 us
  other arithmetic: 80.4 us -> 10.9 us
    pallas_call x0 -> x3, Pallas kernels: none -> 463 us  [the longest x1 384 us: gather_blocks(): pl.pallas_call(kernel, out_shape=jax.ShapeDtypeStruct((count,) + source.s...]
    dot_general x28 -> x3, matrix products: 118 us -> 16.1 us  [outer_sum(): return lax.dot_general(left, right, TN, preferred_element_type=F32)]
    reshape x9 -> x5, local copies, waits for them, and re-layouts: 39.4 us -> 1.12 us  [the longest x1 0.69 us: body(): jnp.sum(jnp.where(hit, places[:, :, None], 0), axis=1).reshape(-1)]
    dynamic_update_slice x4 -> x0, other arithmetic: 36.7 us -> none  [body(): lax.map(forward_group, (queries, all_keys, all_values, live_row))]
    dynamic_update_slice x14 -> x0, local copies, waits for them, and re-layouts: 29 us -> none  [the longest x6 28.3 us: body(): lax.map(backward_group, (queries, all_keys, all_values, soft_probs, soft_...]
    convert_element_type x1 -> x0, local copies, waits for them, and re-layouts: 21.9 us -> none  [body(): outgoing = jnp.einsum('dcs,bsnw->bdcnw', chooser, past_tokens, preferred_...]
    dynamic_slice x15 -> x0, local copies, waits for them, and re-layouts: 21.3 us -> none  [the longest x14 21.3 us: body(): lax.map(forward_group, (queries, all_keys, all_values, live_row))]
    another operation x4 -> x0, other arithmetic: 20.6 us -> none
  transfers between devices with their start and end apart: 3 -> 3, of which waited for: 2 -> 2; matrix products, arithmetic and copies ran while one was open for 5% -> 4% of each run, Pallas kernels for 0% -> 0%
where the time goes in v1:
time: 1080 us
  waiting for transfers between devices  542 us (50%)
  Pallas kernels  463 us (43%)
  matrix products  16.1 us (1%)
  starting transfers between devices  15.5 us (1%)
  between operations  14.2 us (1%)
  local copies, waits for them, and re-layouts  13.9 us (1%)
  other arithmetic  10.9 us (1%)
    pallas_call x1, Pallas kernels, gather_blocks(): pl.pallas_call(kernel, out_shape=jax.ShapeDtypeStruct((count,) + source.s...  384 us
    psum x1, waiting for transfers between devices, body(): lax.psum((grad_pair, grad_wq, grad_wo), ('dp', 'patch'))  314 us
    all_to_all x1, waiting for transfers between devices, body(): lax.all_to_all(outgoing, 'patch', split_axis=0, concat_axis=0, tiled=True)  228 us
    pallas_call x1, Pallas kernels, layer(): pl.pallas_call(kernel, out_shape=(shape(patches, block, width), shape(pat...  70.6 us
  transfers between devices with their start and end apart: 3, of which 2 were waited for; matrix products, arithmetic and copies ran while one was open for 4% of the time, Pallas kernels for 0%

profile of v1, /device:TPU:1, one launch (start us, length us, event | category | flops | bytes accessed | tf_op | source)
XLA Modules:
  0.0 1076.0 jit_solution(7602464482635811301)
XLA Ops:
  7.2 0.8 copy.51
  8.0 0.1 reshape.58
  8.2 0.1 copy.56
  8.3 0.8 copy.57
  9.1 0.1 broadcast_in_dim.29
  9.3 0.2 convert_reduce_fusion
  9.5 0.1 copy.59
  9.6 0.7 reshape.60.index_ref.target_ref
  10.3 383.5 %gather_blocks.1 = bf16[64,128,768]{2,1,0:T(8,128)(2,1)} custom-call(s32[64]{0:T(128)} %reshape.60.index_ref.target_ref, bf16[8,128,768]{2,1,0:T(8,128)(2,1)} %bitcast.23), custom_call_target="tpu_custom_call" | custom-call | tf_op jit(solution)/shard_map/gather_blocks/pallas_call | solution.py:40
  393.9 10.1 all-to-all-start
  403.9 0.1 copy.55
  404.1 0.1 reshape.59
  404.2 0.7 add_reduce_fusion.position_ref
  404.9 0.5 fusion.1.live_ref
  405.4 1.6 pad_maximum_fusion.wkv_ref
  407.0 228.4 %all-to-all-done.arrived_ref = bf16[64,128,768]{2,1,0:T(8,128)(2,1)} async-done(((bf16[64,128,768]{2,1,0:T(8,128)(2,1)}), bf16[64,128,768]{2,1,0:T(8,128)(2,1)}, u32[]{:S(2)}, u32[]{:S(2)}) %all-to-all-start) | async-done | bytes 12582944 | tf_op jit(solution)/shard_map/all_to_all | solution.py:285
  635.4 70.6 %layer.1 = (bf16[2,128,768]{2,1,0:T(8,128)(2,1)}, bf16[2,128,768]{2,1,0:T(8,128)(2,1)}, bf16[64,128,768]{2,1,0:T(8,128)(2,1)}, bf16[2,1664,768]{2,1,0:T(8,128)(2...) custom-call(s32[24]{0:T(128)} %add_reduce_fusion.position_ref, ...), custom_call_target="tpu_custom_call" | custom-call | tf_op jit(solution)/shard_map/layer/pallas_call | solution.py:218
  706.0 5.2 all-to-all-start.1
  711.2 0.2 all-reduce.3.cloned.1.call-start
  711.5 1.9 convolution_bitcast_fusion.1
  713.4 1.9 fusion.2
  715.4 12.2 %convolution_bitcast_fusion = f32[768,1536]{0,1:T(8,128)} fusion(bf16[2,1664,768]{2,1,0:T(8,128)(2,1)S(1)} %copy-done.8, bf16[2,1664,1536]{2,1,0:T(8,128)(2,1)} %get-tuple-element.19), kind=kOutput, calls=%fused_computation | convolution fusion | flops 7851737088 | bytes 20054016 | tf_op jit(solution)/shard_map/dot_general | solution.py:260
  727.6 0.1 copy.60
  727.7 0.1 reshape.61.used_ref
  727.8 314.0 %all-reduce.3.cloned.1.call-done = (f32[768,768]{0,1:T(8,128)}, f32[768,1536]{0,1:T(8,128)}, f32[768,768]{0,1:T(8,128)}) async-done(((f32[768,768]{0,1:T(8,128)}, f32[768,1536]{0,1:T(8,128)}, f32[768,768]{0,1:T(8,128)}), (f32[768,768]{0,1:T(8,128)}, f32[768,1536]{0,1:T(8,128)}, f32[768,768]{0,1:T(8,128)})) %all-reduce.3.cloned.1.call-update) | async-done | bytes 9437200 | tf_op jit(solution)/shard_map/psum | solution.py:296
  1041.8 4.2 broadcast_multiply_fusion
  1046.0 3.0 copy.67
  1049.0 1.9 copy.64
  1051.0 4.2 slice_multiply_fusion
  1055.1 3.0 copy.66
  1058.2 1.9 copy.65
  1060.1 9.0 scatter_sum.1
  (25 shorter events, 0.3 us)
Async XLA Ops:
  393.8 10.1 copy-start.7
  393.8 11.6 %copy-start.3 = (bf16[768,768]{1,0:T(8,128)(2,1)S(1)}, bf16[768,768]{1,0:T(8,128)(2,1)}, u32[]{:S(2)}) copy-start(bf16[768,768]{1,0:T(8,128)(2,1)} %param.17) | copy-start | bytes 3538948
  393.9 11.6 %copy-start.4 = (bf16[768,768]{1,0:T(8,128)(2,1)S(1)}, bf16[768,768]{1,0:T(8,128)(2,1)}, u32[]{:S(2)}) copy-start(bf16[768,768]{1,0:T(8,128)(2,1)} %param.16) | copy-start | bytes 3538948
  393.9 241.5 %all-to-all-start = ((bf16[64,128,768]{2,1,0:T(8,128)(2,1)}), bf16[64,128,768]{2,1,0:T(8,128)(2,1)}, u32[]{:S(2)}, u32[]{:S(2)}) async-start(bf16[64,128,768]{2,1,0:T(8,128)(2,1)} %gather_blocks.1), calls=%async_computation | async-start | bytes 25165824 | tf_op jit(solution)/shard_map/all_to_all | solution.py:285
  706.0 5.5 copy-start.1
  706.0 5.5 copy-start.6
  706.0 354.1 %all-to-all-start.1 = ((bf16[64,128,768]{2,1,0:T(8,128)(2,1)}), bf16[64,128,768]{2,1,0:T(8,128)(2,1)}, u32[]{:S(2)}, u32[]{:S(2)}) async-start(bf16[64,128,768]{2,1,0:T(8,128)(2,1)} %get-tuple-element.16), calls=%async_computation.1 | async-start | bytes 25165824 | tf_op jit(solution)/shard_map/all_to_all | solution.py:290
  711.2 2.2 copy-start.2
  711.2 2.2 copy-start.5
  711.2 330.6 %all-reduce.3.cloned.1.call-start = ((), (), s32[]{:S(2)}) async-start(), calls=%async_computation.2 | async-start | bytes 18874368 | tf_op jit(solution)/shard_map/psum | solution.py:296
  711.5 3.9 copy-start.8
  1058.2 1.9 copy-start
Sparse Core Ops, SparseCore 0:
  727.7 314.0 all-reduce.2

commit v2 on v1

--- a/solution.py
+++ b/solution.py
@@ -10,6 +10,7 @@
 H = 12
 HD = 64
 F32 = jnp.float32
+MESH = pl.DeviceIdType.MESH
 BF16 = jnp.bfloat16
 NN = (((1,), (0,)), ((), ()))
 NT = (((1,), (1,)), ((), ()))
@@ -20,35 +21,348 @@
     return lax.dot_general(a, b, dims, preferred_element_type=F32)
 
 
-def gather_blocks(source, index):
-    count = index.shape[0]
-
-    def kernel(index_ref, source_ref, out_ref, sems):
-        def copy(i):
+def place():
+    device = lax.axis_index("patch")
+    return device // 8, (device // 4) % 2, device % 4, lax.axis_index("dp")
+
+
+def step_id(y, x, z, dim, hop):
+    return ((y + hop * (1 - dim)) % 4) * 8 + x * 4 + (z + hop * dim) % 4
+
+
+def meet(y, x, z, dp, across):
+    barrier = pltpu.get_barrier_semaphore()
+    ids = [step_id(y, x, z, dim, hop) for dim in (0, 1) for hop in (1, 2, 3)]
+    if across:
+        ids.append(y * 8 + (1 - x) * 4 + z)
+    for other in ids:
+        pl.semaphore_signal(barrier, 1, device_id=(dp, other), device_id_type=MESH)
+    pl.semaphore_wait(barrier, len(ids))
+
+
+def spread(past, table):
+    blocks, rows, width = past.shape
+    chunk = blocks // 2
+    cap = 8
+
+    def kernel(
+        table_ref, past_ref, out_ref, have_a, have_b, sel_a, sel_b,
+        in_sem, x_send, x_recv, g_send, g_recv, e_send, e_recv, own_sem,
+    ):
+        y, x, z, dp = place()
+        pos = lambda dim, hop=0: (y * (1 - dim) + z * dim + hop) % 4
+        have, sel = (have_a, have_b), (sel_a, sel_b)
+        half = (x, 1 - x)
+
+        def region(t, hop, c):
+            return have[t].at[pl.ds(pos(half[t], hop) * blocks + c * chunk, chunk)]
+
+        local = pltpu.make_async_copy(
+            past_ref, have_a.at[pl.ds(pos(half[0]) * blocks, blocks)], in_sem
+        )
+        local.start()
+        meet(y, x, z, dp, True)
+
+        def cross(c):
+            at = pl.ds(pos(half[0]) * blocks + c * chunk, chunk)
+            return pltpu.make_async_remote_copy(
+                past_ref.at[pl.ds(c * chunk, chunk)], have_b.at[at], x_send.at[c], x_recv.at[c],
+                device_id=(dp, y * 8 + (1 - x) * 4 + z), device_id_type=MESH,
+            )
+
+        def crossed(c):
+            at = pl.ds(pos(half[1]) * blocks + c * chunk, chunk)
+            return pltpu.make_async_remote_copy(
+                past_ref.at[pl.ds(c * chunk, chunk)], have_b.at[at], x_send.at[c], x_recv.at[c],
+                device_id=(dp, y * 8 + (1 - x) * 4 + z), device_id_type=MESH,
+            )
+
+        ways = ((1, 0, 0), (3, 0, 1), (1, 0, 1), (3, 0, 0), (1, 3, 0), (3, 1, 1))
+
+        def go(t, n):
+            way, owner, c = ways[n]
+            return pltpu.make_async_remote_copy(
+                region(t, owner, c), region(t, owner, c), g_send.at[t, n], g_recv.at[t, n],
+                device_id=(dp, step_id(y, x, z, half[t], way)), device_id_type=MESH,
+            )
+
+        def came(t, n):
+            way, owner, c = ways[n]
+            owner = (owner - way) % 4
+            return pltpu.make_async_remote_copy(
+                region(t, owner, c), region(t, owner, c), g_send.at[t, n], g_recv.at[t, n],
+                device_id=(dp, step_id(y, x, z, half[t], way)), device_id_type=MESH,
+            )
+
+        def swap(t, hop, arriving=False):
+            h = half[t]
+            at = h * 4 + pos(1 - h, -hop if arriving else 0)
+            return pltpu.make_async_remote_copy(
+                sel[t].at[hop], out_ref.at[pl.ds(at * cap, cap)],
+                e_send.at[t, hop - 1], e_recv.at[t, hop - 1],
+                device_id=(dp, step_id(y, x, z, 1 - h, hop)), device_id_type=MESH,
+            )
+
+        def keep(t):
+            h = half[t]
+            at = h * 4 + pos(1 - h)
             return pltpu.make_async_copy(
-                source_ref.at[index_ref[i]], out_ref.at[i], sems.at[i]
-            )
-
-        @pl.loop(0, count)
-        def _(i):
-            copy(i).start()
-
-        @pl.loop(0, count)
-        def _(i):
-            copy(i).wait()
+                sel[t].at[0], out_ref.at[pl.ds(at * cap, cap)], own_sem.at[t]
+            )
+
+        def choose(t):
+            h = half[t]
+            for hop in (2, 1, 3, 0):
+                row = h * 4 + pos(1 - h, hop)
+
+                @pl.loop(0, cap)
+                def _(s):
+                    sel[t][hop, s] = have[t][table_ref[row * cap + s]]
+
+                if hop:
+                    swap(t, hop).start()
+                else:
+                    keep(t).start()
+
+        cross(0).start()
+        cross(1).start()
+        local.wait()
+        for n in range(4):
+            go(0, n).start()
+        crossed(0).wait_recv()
+        go(1, 0).start()
+        go(1, 3).start()
+        came(0, 0).wait_recv()
+        go(0, 4).start()
+        came(0, 1).wait_recv()
+        go(0, 5).start()
+        crossed(1).wait_recv()
+        go(1, 1).start()
+        go(1, 2).start()
+        for n in (2, 3, 4, 5):
+            came(0, n).wait_recv()
+        choose(0)
+        came(1, 0).wait_recv()
+        go(1, 4).start()
+        came(1, 1).wait_recv()
+        go(1, 5).start()
+        for n in (2, 3, 4, 5):
+            came(1, n).wait_recv()
+        choose(1)
+        for t in (0, 1):
+            for hop in (1, 2, 3):
+                swap(t, hop, True).wait_recv()
+            keep(t).wait()
+        for t in (0, 1):
+            cross(t).wait_send()
+            for n in range(6):
+                go(t, n).wait_send()
+            for hop in (1, 2, 3):
+                swap(t, hop).wait_send()
 
     return pl.pallas_call(
         kernel,
-        out_shape=jax.ShapeDtypeStruct((count,) + source.shape[1:], source.dtype),
-        grid_spec=pltpu.PrefetchScalarGridSpec(
-            num_scalar_prefetch=1,
-            grid=(),
-            in_specs=[pl.BlockSpec(memory_space=pl.ANY)],
-            out_specs=pl.BlockSpec(memory_space=pl.ANY),
-            scratch_shapes=[pltpu.SemaphoreType.DMA((count,))],
+        out_shape=jax.ShapeDtypeStruct((8 * cap, rows, width), past.dtype),
+        in_specs=[pl.BlockSpec(memory_space=pltpu.SMEM), pl.BlockSpec(memory_space=pl.ANY)],
+        out_specs=pl.BlockSpec(memory_space=pl.ANY),
+        scratch_shapes=[
+            pltpu.VMEM((4 * blocks, rows, width), past.dtype),
+            pltpu.VMEM((4 * blocks, rows, width), past.dtype),
+            pltpu.VMEM((4, cap, rows, width), past.dtype),
+            pltpu.VMEM((4, cap, rows, width), past.dtype),
+            pltpu.SemaphoreType.DMA,
+            pltpu.SemaphoreType.DMA((2,)),
+            pltpu.SemaphoreType.DMA((2,)),
+            pltpu.SemaphoreType.DMA((2, 6)),
+            pltpu.SemaphoreType.DMA((2, 6)),
+            pltpu.SemaphoreType.DMA((2, 3)),
+            pltpu.SemaphoreType.DMA((2, 3)),
+            pltpu.SemaphoreType.DMA((2,)),
+        ],
+        compiler_params=pltpu.CompilerParams(
+            collective_id=0, has_side_effects=True, vmem_limit_bytes=48 << 20
         ),
-        name="gather_blocks",
-    )(index, source)
+        name="spread",
+    )(table, past)
+
+
+def send_back(grads):
+    slots, rows, width = grads.shape
+    cap = slots // 8
+
+    def kernel(grad_ref, out_ref, own, send, recv, own_sem):
+        y, x, z, dp = place()
+        pos = lambda dim, hop=0: (y * (1 - dim) + z * dim + hop) % 4
+        part = lambda ref, at: ref.at[pl.ds(at * cap, cap)]
+
+        def swap(h, hop, arriving=False):
+            return pltpu.make_async_remote_copy(
+                part(grad_ref, h * 4 + pos(1 - h, hop)),
+                part(out_ref, h * 4 + pos(1 - h, -hop if arriving else 0)),
+                send.at[h, hop - 1], recv.at[h, hop - 1],
+                device_id=(dp, step_id(y, x, z, 1 - h, hop)), device_id_type=MESH,
+            )
+
+        def load(h):
+            return pltpu.make_async_copy(
+                part(grad_ref, h * 4 + pos(1 - h)), own.at[h], own_sem.at[h]
+            )
+
+        def store(h):
+            return pltpu.make_async_copy(
+                own.at[h], part(out_ref, h * 4 + pos(1 - h)), own_sem.at[h]
+            )
+
+        for h in (0, 1):
+            load(h).start()
+        meet(y, x, z, dp, False)
+        for hop in (2, 1, 3):
+            for h in (0, 1):
+                swap(h, hop).start()
+        for h in (0, 1):
+            load(h).wait()
+            store(h).start()
+        for h in (0, 1):
+            store(h).wait()
+            for hop in (1, 2, 3):
+                swap(h, hop, True).wait_recv()
+        for h in (0, 1):
+            for hop in (1, 2, 3):
+                swap(h, hop).wait_send()
+
+    return pl.pallas_call(
+        kernel,
+        out_shape=jax.ShapeDtypeStruct(grads.shape, grads.dtype),
+        in_specs=[pl.BlockSpec(memory_space=pl.ANY)],
+        out_specs=pl.BlockSpec(memory_space=pl.ANY),
+        scratch_shapes=[
+            pltpu.VMEM((2, cap, rows, width), grads.dtype),
+            pltpu.SemaphoreType.DMA((2, 3)),
+            pltpu.SemaphoreType.DMA((2, 3)),
+            pltpu.SemaphoreType.DMA((2,)),
+        ],
+        compiler_params=pltpu.CompilerParams(
+            collective_id=1, has_side_effects=True, vmem_limit_bytes=32 << 20
+        ),
+        name="send_back",
+    )(grads)
+
+
+def collect(partial):
+    groups, blocks, rows, width = partial.shape
+    chunk = blocks // 2
+
+    def kernel(
+        part_ref, out_ref, relay, staged, inward, mine, across,
+        r_send, r_recv, d_send, d_recv, x_send, x_recv,
+    ):
+        y, x, z, dp = place()
+        pos = lambda dim, hop=0: (y * (1 - dim) + z * dim + hop) % 4
+        half = (1 - x, x)
+        meet(y, x, z, dp, True)
+        ways = (3, 1)
+
+        def row(t, hop):
+            return half[t] * 4 + pos(half[t], hop)
+
+        def pass_on(t, side):
+            return pltpu.make_async_remote_copy(
+                part_ref.at[row(t, 2), pl.ds(side * chunk, chunk)], relay.at[t, side],
+                r_send.at[t, side], r_recv.at[t, side],
+                device_id=(dp, step_id(y, x, z, half[t], ways[side])), device_id_type=MESH,
+            )
+
+        def direct(t, side, summed):
+            c = side if summed else 1 - side
+            source = (
+                staged.at[t, side] if summed
+                else part_ref.at[row(t, ways[side]), pl.ds(c * chunk, chunk)]
+            )
+            return pltpu.make_async_remote_copy(
+                source, inward.at[t, side, pl.ds(c * chunk, chunk)],
+                d_send.at[t, side, int(summed)], d_recv.at[t, side, int(summed)],
+                device_id=(dp, step_id(y, x, z, half[t], ways[side])), device_id_type=MESH,
+            )
+
+        def cross(c):
+            return pltpu.make_async_remote_copy(
+                mine.at[pl.ds(c * chunk, chunk)], across.at[pl.ds(c * chunk, chunk)],
+                x_send.at[c], x_recv.at[c],
+                device_id=(dp, y * 8 + (1 - x) * 4 + z), device_id_type=MESH,
+            )
+
+        def final(t, b):
+            return (
+                part_ref[row(t, 0), b].astype(F32)
+                + inward[t, 0, b].astype(F32)
+                + inward[t, 1, b].astype(F32)
+            )
+
+        for t in (0, 1):
+            for side in (0, 1):
+                pass_on(t, side).start()
+        for t in (0, 1):
+            for side in (0, 1):
+                direct(t, side, False).start()
+        for t in (0, 1):
+            for side in (0, 1):
+                pass_on(t, side).wait_recv()
+
+                @pl.loop(0, chunk)
+                def _(b):
+                    own = part_ref[row(t, ways[side]), side * chunk + b]
+                    staged[t, side, b] = (
+                        own.astype(F32) + relay[t, side, b].astype(F32)
+                    ).astype(staged.dtype)
+
+                direct(t, side, True).start()
+        for side in (0, 1):
+            for summed in (False, True):
+                direct(0, side, summed).wait_recv()
+        for c in (0, 1):
+            @pl.loop(0, chunk)
+            def _(b):
+                mine[c * chunk + b] = final(0, c * chunk + b).astype(mine.dtype)
+
+            cross(c).start()
+        for side in (0, 1):
+            for summed in (False, True):
+                direct(1, side, summed).wait_recv()
+        for c in (0, 1):
+            cross(c).wait_recv()
+
+            @pl.loop(0, chunk)
+            def _(b):
+                at = c * chunk + b
+                out_ref[at] = (final(1, at) + across[at].astype(F32)).astype(out_ref.dtype)
+
+        for t in (0, 1):
+            cross(t).wait_send()
+            for side in (0, 1):
+                pass_on(t, side).wait_send()
+                for summed in (False, True):
+                    direct(t, side, summed).wait_send()
+
+    shape = lambda *s: pltpu.VMEM(s + (rows, width), partial.dtype)
+    return pl.pallas_call(
+        kernel,
+        out_shape=jax.ShapeDtypeStruct((blocks, rows, width), partial.dtype),
+        in_specs=[pl.BlockSpec(memory_space=pltpu.VMEM)],
+        out_specs=pl.BlockSpec(memory_space=pltpu.VMEM),
+        scratch_shapes=[
+            shape(2, 2, chunk), shape(2, 2, chunk), shape(2, 2, blocks), shape(blocks), shape(blocks),
+            pltpu.SemaphoreType.DMA((2, 2)),
+            pltpu.SemaphoreType.DMA((2, 2)),
+            pltpu.SemaphoreType.DMA((2, 2, 2)),
+            pltpu.SemaphoreType.DMA((2, 2, 2)),
+            pltpu.SemaphoreType.DMA((2,)),
+            pltpu.SemaphoreType.DMA((2,)),
+        ],
+        compiler_params=pltpu.CompilerParams(
+            collective_id=2, has_side_effects=True, vmem_limit_bytes=48 << 20
+        ),
+        name="collect",
+    )(partial)
 
 
 def scatter_sum(source, target, used, outputs):
@@ -267,30 +581,37 @@
     _, patches, block, width = query_tokens.shape
     tokens, grads, past = query_tokens[0], grad_out[0], past_tokens[0]
     peers = lax.axis_size("patch")
-    device = lax.axis_index("patch")
+    y, x, z, _ = place()
     per_device = patches * source_dev.shape[1] * source_dev.shape[2]
-    cap = 2
-    owners = source_dev.reshape(peers, per_device)
-    places = source_slot.reshape(peers, per_device)
+    cap = 8
+
+    grid = lambda a: a.reshape(4, 2, 4, per_device)
+    near = lambda a: jnp.concatenate([grid(a)[y, x], grid(a)[:, x, z]], axis=0)
+    owner, slot = near(source_dev), near(source_slot)
+    from_y, half, from_z = owner // 8, (owner // 4) % 2, owner % 4
+    key = half * 4 + jnp.where(half == 0, from_z, from_y)
+    number = jnp.where(half == 0, from_y, from_z) * past.shape[0] + slot
     order = jnp.arange(per_device)
-    matches = (owners[:, :, None] == owners[:, None, :]) & (order[:, None] > order[None, :])
+    matches = (key[:, :, None] == key[:, None, :]) & (order[:, None] > order[None, :])
     rank = jnp.sum(matches.astype(jnp.int32), axis=2)
-    hit = (rank[:, :, None] == jnp.arange(cap)) & (owners == device)[:, :, None]
-    out_place = jnp.sum(jnp.where(hit, places[:, :, None], 0), axis=1).reshape(-1)
-    out_used = jnp.sum(hit.astype(jnp.int32), axis=1).reshape(-1)
-    mine = owners[device] * cap + rank[device]
-    live = kept.reshape(peers, per_device)[device]
-
-    outgoing = gather_blocks(past, out_place)
-    arrived = lax.all_to_all(outgoing, "patch", split_axis=0, concat_axis=0, tiled=True)
+    chosen_here = jnp.where(jnp.arange(8) < 4, z, 4 + y)
+    hit = (rank[:, :, None] == jnp.arange(cap)) & (key == chosen_here[:, None])[:, :, None]
+    table = jnp.sum(jnp.where(hit, number[:, :, None], 0), axis=1)
+    used = jnp.sum(hit.astype(jnp.int32), axis=1).reshape(-1)
+    target = (table + jnp.where(jnp.arange(8) < 4, 0, 4 * past.shape[0])[:, None]).reshape(-1)
+    mine = key[z] * cap + rank[z]
+    live = grid(kept)[y, x, z]
+
+    arrived = spread(past, table.reshape(-1))
     w_pair = jnp.concatenate([w_key, w_value], axis=1)
-    attn, token_grad, far_grad, x, dkv, dq, mixed = layer(
-        mine, live, arrived, tokens, grads, w_query, w_pair, w_out, peers * cap
+    attn, token_grad, far_grad, seen, dkv, dq, mixed = layer(
+        mine, live, arrived, tokens, grads, w_query, w_pair, w_out, 8 * cap
     )
-    returned = lax.all_to_all(far_grad, "patch", split_axis=0, concat_axis=0, tiled=True)
-    past_grad = scatter_sum(returned, out_place, out_used, past.shape[0])
+    returned = send_back(far_grad)
+    partial = scatter_sum(returned, target, used, 8 * past.shape[0])
+    past_grad = collect(partial.reshape((8,) + past.shape))
     flat = lambda a: a.reshape(-1, a.shape[-1])
-    grad_pair = outer_sum(flat(x), flat(dkv))
+    grad_pair = outer_sum(flat(seen), flat(dkv))
     grad_wq = outer_sum(flat(tokens), flat(dq))
     grad_wo = outer_sum(flat(mixed), flat(grads))
     grad_pair, grad_wq, grad_wo = lax.psum((grad_pair, grad_wq, grad_wo), ("dp", "patch"))

time: 1080 us -> 575 us (0.53)
  waiting for transfers between devices: 542 us -> 8.17 us
  Pallas kernels: 463 us -> 497 us
  starting transfers between devices: 15.5 us -> 0.04 us
    psum x1, waiting for transfers between devices: 314 us -> 8.16 us  [body(): lax.psum((grad_pair, grad_wq, grad_wo), ('dp', 'patch'))]
    all_to_all x2 -> x0, waiting for transfers between devices: 228 us -> none  [the longest x1 228 us: body(): lax.all_to_all(outgoing, 'patch', split_axis=0, concat_axis=0, tiled=True)]
    pallas_call x1 -> x3, Pallas kernels: 384 us -> 411 us  [the longest x1 216 us: spread(): pl.pallas_call(kernel, out_shape=jax.ShapeDtypeStruct((8 * cap, rows, wid...]
    all_to_all x2 -> x0, starting transfers between devices: 15.3 us -> none  [the longest x1 10.1 us: body(): lax.all_to_all(outgoing, 'patch', split_axis=0, concat_axis=0, tiled=True)]
  transfers between devices with their start and end apart: 3 -> 1, of which waited for: 2 -> 1; matrix products, arithmetic and copies ran while one was open for 4% -> 0% of each run, Pallas kernels for 0% -> 37%
where the time goes in v2:
time: 575 us; the launch traced here: 574 us
  Pallas kernels  497 us (86%)
  local copies, waits for them, and re-layouts  21.6 us (4%)
  matrix products  17.2 us (3%)
  other arithmetic  16.1 us (3%)
  between operations  14.3 us (2%)
  waiting for transfers between devices  8.17 us (1%)
    pallas_call x1, Pallas kernels, spread(): pl.pallas_call(kernel, out_shape=jax.ShapeDtypeStruct((8 * cap, rows, wid...  216 us
    pallas_call x1, Pallas kernels, collect(): pl.pallas_call(kernel, out_shape=jax.ShapeDtypeStruct((blocks, rows, widt...  108 us
    pallas_call x1, Pallas kernels, send_back(): pl.pallas_call(kernel, out_shape=jax.ShapeDtypeStruct(grads.shape, grads....  86.5 us
    pallas_call x1, Pallas kernels, layer(): pl.pallas_call(kernel, out_shape=(shape(patches, block, width), shape(pat...  70.8 us
    unnamed x20, local copies, waits for them, and re-layouts  20.3 us
    dot_general x3, matrix products, outer_sum(): return lax.dot_general(left, right, TN, preferred_element_type=F32)  17.2 us
    pallas_call x1, Pallas kernels, scatter_sum(): pl.pallas_call(kernel, out_shape=jax.ShapeDtypeStruct((outputs, rows, wid...  15.1 us
  transfers between devices with their start and end apart: 1, of which 1 were waited for; matrix products, arithmetic and copies ran while one was open for 0% of the time, Pallas kernels for 37%

profile of v2, /device:TPU:1, one launch (start us, length us, event | category | flops | bytes accessed | tf_op | source)
XLA Modules:
  0.0 574.1 jit_solution(16431994638768348274)
XLA Ops:
  7.3 0.8 copy.34
  8.1 0.1 reshape.501
  8.3 0.8 copy.36
  9.1 0.1 reshape.503
  9.4 0.3 convert_reduce_fusion
  9.7 0.5 fusion.8.position_ref
  10.2 0.3 convert_reduce_fusion.1
  10.5 0.1 reshape.504.table_ref
  10.6 0.8 copy.35
  11.5 0.1 reshape.502
  11.6 0.5 fusion.7.live_ref
  12.1 3.3 pad_maximum_fusion.wkv_ref
  15.4 216.0 %spread.1.arrived_ref = bf16[64,128,768]{2,1,0:T(8,128)(2,1)} custom-call(s32[64]{0:T(128)S(1)} %reshape.504.table_ref, bf16[8,128,768]{2,1,0:T(8,128)(2,1)S(1)} %bitcast.32), custom_call_target="tpu_custom_call" | custom-call | tf_op jit(solution)/shard_map/spread/pallas_call | solution.py:163
  231.4 70.8 %layer.1 = (bf16[2,128,768]{2,1,0:T(8,128)(2,1)}, bf16[2,128,768]{2,1,0:T(8,128)(2,1)}, bf16[64,128,768]{2,1,0:T(8,128)(2,1)}, bf16[2,1664,768]{2,1,0:T(8,128)(2...) custom-call(s32[24]{0:T(128)} %fusion.8.position_ref, ...), custom_call_target="tpu_custom_call" | custom-call | tf_op jit(solution)/shard_map/layer/pallas_call | solution.py:532
  302.2 3.1 convolution_bitcast_fusion.1
  305.3 1.9 fusion.9
  307.2 12.2 %convolution_bitcast_fusion = f32[768,1536]{0,1:T(8,128)} fusion(bf16[2,1664,768]{2,1,0:T(8,128)(2,1)S(1)} %copy-done.5, bf16[2,1664,1536]{2,1,0:T(8,128)(2,1)} %get-tuple-element.19), kind=kOutput, calls=%fused_computation | convolution fusion | flops 7851737088 | bytes 20054016 | tf_op jit(solution)/shard_map/dot_general | solution.py:574
  319.6 0.1 add.155
  319.7 0.1 reshape.505.used_ref
  319.8 86.5 %send_back.1.source_ref = bf16[64,128,768]{2,1,0:T(8,128)(2,1)S(1)} custom-call(bf16[64,128,768]{2,1,0:T(8,128)(2,1)} %get-tuple-element.16.grad_ref), custom_call_target="tpu_custom_call" | custom-call | tf_op jit(solution)/shard_map/send_back/pallas_call | solution.py:233
  406.3 4.5 copy-done
  410.8 15.1 %scatter_sum.1 = bf16[64,128,768]{2,1,0:T(8,128)(2,1)} custom-call(s32[64]{0:T(128)S(1)} %add.156.target_ref, s32[64]{0:T(128)S(1)} %reshape.505.used_ref, bf16[64,128,768]{2,1,0:T(8,128)(2,1)} %copy-done), custom_call_target="tpu_custom_call" | custom-call | tf_op jit(solution)/shard_map/scatter_sum/pallas_call | solution.py:389
  425.9 108.4 %collect.1 = bf16[8,128,768]{2,1,0:T(8,128)(2,1)S(1)} custom-call(bf16[8,8,128,768]{3,2,1,0:T(8,128)(2,1)} %bitcast.33), custom_call_target="tpu_custom_call" | custom-call | tf_op jit(solution)/shard_map/collect/pallas_call | solution.py:347
  534.3 8.2 %all-reduce.3.cloned.1.call-done = (f32[768,768]{0,1:T(8,128)}, f32[768,1536]{0,1:T(8,128)}, f32[768,768]{0,1:T(8,128)}) async-done(((f32[768,768]{0,1:T(8,128)}, f32[768,1536]{0,1:T(8,128)}, f32[768,768]{0,1:T(8,128)}), (f32[768,768]{0,1:T(8,128)}, f32[768,1536]{0,1:T(8,128)}, f32[768,768]{0,1:T(8,128)})) %all-reduce.3.cloned.1.call-update) | async-done | bytes 9437200 | tf_op jit(solution)/shard_map/psum | solution.py:617
  542.4 3.3 broadcast_multiply_fusion.1
  545.7 3.0 copy.40
  548.8 3.3 broadcast_multiply_fusion
  552.0 3.0 copy.43
  555.1 5.0 slice_multiply_fusion
  560.0 3.0 copy.42
  563.1 3.0 copy.41
  566.1 1.1 copy.52
  (22 shorter events, 0.3 us)
Async XLA Ops:
  7.2 535.3 %all-reduce.3.cloned.1.call-start = ((), (), s32[]{:S(2)}) async-start(), calls=%async_computation | async-start | bytes 18874368 | tf_op jit(solution)/shard_map/psum | solution.py:617
  12.1 3.3 copy-start.1
  231.4 70.8 %copy-start.2 = (bf16[1,2,128,768]{3,2,1,0:T(8,128)(2,1)S(1)}, bf16[1,2,128,768]{3,2,1,0:T(8,128)(2,1)}, u32[]{:S(2)}) copy-start(bf16[1,2,128,768]{3,2,1,0:T(8,128)(2,1)} %param.10) | copy-start | bytes 1179652
  302.2 3.1 copy-start.3
  302.2 3.1 copy-start.4
  302.2 5.0 copy-start.5
  406.2 4.5 copy-start
Sparse Core Ops, SparseCore 0:
  319.6 222.7 all-reduce.2

commit v3 on v2

--- a/solution.py
+++ b/solution.py
@@ -141,13 +141,13 @@
         go(1, 2).start()
         for n in (2, 3, 4, 5):
             came(0, n).wait_recv()
-        choose(0)
         came(1, 0).wait_recv()
         go(1, 4).start()
         came(1, 1).wait_recv()
         go(1, 5).start()
         for n in (2, 3, 4, 5):
             came(1, n).wait_recv()
+        choose(0)
         choose(1)
         for t in (0, 1):
             for hop in (1, 2, 3):
@@ -611,19 +611,23 @@
     partial = scatter_sum(returned, target, used, 8 * past.shape[0])
     past_grad = collect(partial.reshape((8,) + past.shape))
     flat = lambda a: a.reshape(-1, a.shape[-1])
-    grad_pair = outer_sum(flat(seen), flat(dkv))
-    grad_wq = outer_sum(flat(tokens), flat(dq))
-    grad_wo = outer_sum(flat(mixed), flat(grads))
-    grad_pair, grad_wq, grad_wo = lax.psum((grad_pair, grad_wq, grad_wo), ("dp", "patch"))
     scale = 1.0 / math.sqrt(lax.axis_size("dp") * peers * patches * block)
+    dkv, seen = flat(dkv), flat(seen)
+    grad_wk = outer_sum(seen, dkv[:, :width]) * scale
+    grad_wv = outer_sum(seen, dkv[:, width:]) * scale
+    grad_wq = outer_sum(flat(tokens), flat(dq)) * scale
+    grad_wo = outer_sum(flat(mixed), flat(grads)) * scale
+    grad_wq, grad_wk, grad_wv, grad_wo = lax.psum(
+        (grad_wq, grad_wk, grad_wv, grad_wo), ("dp", "patch")
+    )
     return (
         attn[None],
         token_grad[None],
         past_grad[None],
-        grad_wq * scale,
-        grad_pair[:, :width] * scale,
-        grad_pair[:, width:] * scale,
-        grad_wo * scale,
+        grad_wq,
+        grad_wk,
+        grad_wv,
+        grad_wo,
     )
 
 

time: 575 us -> 495 us (0.86)
  Pallas kernels: 497 us -> 429 us
  other arithmetic: 16.1 us -> 4.59 us
    pallas_call x1, Pallas kernels: 216 us -> 147 us  [spread(): pl.pallas_call(kernel, out_shape=jax.ShapeDtypeStruct((8 * cap, rows, wid...]
    mul x3 -> x0, other arithmetic: 11.5 us -> none  [the longest x1 4.97 us: body(): grad_pair[:, width:] * scale]
    dot_general x3 -> x4, matrix products: 17.2 us -> 19.2 us  [outer_sum(): return lax.dot_general(left, right, TN, preferred_element_type=F32)]
    unnamed x20 -> x30, local copies, waits for them, and re-layouts: 20.3 us -> 18.7 us
  transfers between devices with their start and end apart: 1 -> 1, of which waited for: 1 -> 1; matrix products, arithmetic and copies ran while one was open for 0% -> 0% of each run, Pallas kernels for 37% -> 43%
where the time goes in v3:
time: 495 us
  Pallas kernels  429 us (87%)
  local copies, waits for them, and re-layouts  20 us (4%)
  matrix products  19.2 us (4%)
  between operations  14.3 us (3%)
  waiting for transfers between devices  7.66 us (2%)
    pallas_call x1, Pallas kernels, spread(): pl.pallas_call(kernel, out_shape=jax.ShapeDtypeStruct((8 * cap, rows, wid...  147 us
    pallas_call x1, Pallas kernels, collect(): pl.pallas_call(kernel, out_shape=jax.ShapeDtypeStruct((blocks, rows, widt...  109 us
    pallas_call x1, Pallas kernels, send_back(): pl.pallas_call(kernel, out_shape=jax.ShapeDtypeStruct(grads.shape, grads....  86.8 us
    pallas_call x1, Pallas kernels, layer(): pl.pallas_call(kernel, out_shape=(shape(patches, block, width), shape(pat...  70.7 us
    dot_general x4, matrix products, outer_sum(): return lax.dot_general(left, right, TN, preferred_element_type=F32)  19.2 us
    unnamed x30, local copies, waits for them, and re-layouts  18.7 us
    pallas_call x1, Pallas kernels, scatter_sum(): pl.pallas_call(kernel, out_shape=jax.ShapeDtypeStruct((outputs, rows, wid...  15.2 us
  transfers between devices with their start and end apart: 1, of which 1 were waited for; matrix products, arithmetic and copies ran while one was open for 0% of the time, Pallas kernels for 43%

profile of v3, /device:TPU:1, one launch (start us, length us, event | category | flops | bytes accessed | tf_op | source)
XLA Modules:
  0.0 494.6 jit_solution(8664138594231304697)
XLA Ops:
  7.3 0.8 copy.22
  8.1 0.1 reshape.505
  8.3 0.8 copy.24
  9.1 0.1 reshape.507
  9.4 0.3 convert_reduce_fusion
  9.7 0.5 fusion.18.position_ref
  10.2 0.3 convert_reduce_fusion.1
  10.5 0.1 reshape.508.table_ref
  10.6 0.8 copy.23
  11.5 0.1 reshape.506
  11.6 0.5 fusion.17.live_ref
  12.1 3.3 pad_maximum_fusion.wkv_ref
  15.4 147.3 %spread.1.arrived_ref = bf16[64,128,768]{2,1,0:T(8,128)(2,1)} custom-call(s32[64]{0:T(128)S(1)} %reshape.508.table_ref, bf16[8,128,768]{2,1,0:T(8,128)(2,1)S(1)} %bitcast.32), custom_call_target="tpu_custom_call" | custom-call | tf_op jit(solution)/shard_map/spread/pallas_call | solution.py:163
  162.7 70.7 %layer.1 = (bf16[2,128,768]{2,1,0:T(8,128)(2,1)}, bf16[2,128,768]{2,1,0:T(8,128)(2,1)}, bf16[64,128,768]{2,1,0:T(8,128)(2,1)}, bf16[2,1664,768]{2,1,0:T(8,128)(2...) custom-call(s32[24]{0:T(128)} %fusion.18.position_ref, ...), custom_call_target="tpu_custom_call" | custom-call | tf_op jit(solution)/shard_map/layer/pallas_call | solution.py:532
  233.5 9.8 %fusion.7 = f32[768,768]{1,0:T(8,128)} fusion(bf16[3328,768]{1,0:T(8,128)(2,1)} %bitcast.45, bf16[3328,1536]{1,0:T(8,128)(2,1)} %bitcast.43), kind=kOutput, calls=%fused_computation.7 | convolution fusion | flops 3926458368 | bytes 12582912 | tf_op jit(solution)/shard_map/dot_general | solution.py:574
  243.2 5.6 %fusion.4 = f32[768,768]{1,0:T(8,128)} fusion(bf16[3328,768]{1,0:T(8,128)(2,1)S(1)} %bitcast.46, bf16[3328,1536]{1,0:T(8,128)(2,1)S(1)} %bitcast.44), kind=kOutput, calls=%fused_computation.6 | convolution fusion | flops 3926458368 | bytes 12582912 | tf_op jit(solution)/shard_map/dot_general | solution.py:574
  248.9 1.9 multiply_bitcast_fusion
  250.8 1.9 convolution_multiply_fusion
  252.8 0.1 add.157
  253.0 86.8 %send_back.1.source_ref = bf16[64,128,768]{2,1,0:T(8,128)(2,1)S(1)} custom-call(bf16[64,128,768]{2,1,0:T(8,128)(2,1)} %get-tuple-element.16.grad_ref), custom_call_target="tpu_custom_call" | custom-call | tf_op jit(solution)/shard_map/send_back/pallas_call | solution.py:233
  339.9 4.5 copy-done
  344.4 15.2 %scatter_sum.1 = bf16[64,128,768]{2,1,0:T(8,128)(2,1)} custom-call(s32[64]{0:T(128)S(1)} %add.158.target_ref, s32[64]{0:T(128)S(1)} %reshape.509.used_ref, bf16[64,128,768]{2,1,0:T(8,128)(2,1)} %copy-done), custom_call_target="tpu_custom_call" | custom-call | tf_op jit(solution)/shard_map/scatter_sum/pallas_call | solution.py:389
  359.6 108.8 %collect.1 = bf16[8,128,768]{2,1,0:T(8,128)(2,1)S(1)} custom-call(bf16[8,8,128,768]{3,2,1,0:T(8,128)(2,1)} %bitcast.33), custom_call_target="tpu_custom_call" | custom-call | tf_op jit(solution)/shard_map/collect/pallas_call | solution.py:347
  468.4 7.6 %all-reduce.3.cloned.1.call-done = (f32[768,768]{0,1:T(8,128)}, f32[768,768]{1,0:T(8,128)}, f32[768,768]{1,0:T(8,128)}, f32[768,768]{1,0:T(8,128)}) async-done(((f32[768,768]{0,1:T(8,128)}, f32[768,768]{1,0:T(8,128)}, f32[768,768]{1,0:T(8,128)}, f32[768,768]{1,0:T(8,128)}), (f32[768,768]{0,1:T(8,128)}, f32[768,768]{1,0:T(8,128)}, f32[768,768]{1,0:T(8,128)}, ...) | async-done | bytes 9437200 | tf_op jit(solution)/shard_map/psum | solution.py:620
  476.1 3.0 copy.25
  479.1 1.1 copy.31
  480.3 1.1 copy-done.4
  481.3 1.4 copy.32
  482.7 1.1 copy-done.3
  483.9 1.4 copy.33
  485.3 1.1 copy-done.2
  486.4 1.4 copy.34
  (30 shorter events, 0.4 us)
Async XLA Ops:
  7.2 468.9 %all-reduce.3.cloned.1.call-start = ((), (), s32[]{:S(2)}) async-start(), calls=%async_computation | async-start | bytes 18874368 | tf_op jit(solution)/shard_map/psum | solution.py:620
  12.1 3.3 copy-start.1
  233.4 9.8 %copy-start.9 = (bf16[2,1664,1536]{2,1,0:T(8,128)(2,1)S(1)}, bf16[2,1664,1536]{2,1,0:T(8,128)(2,1)}, u32[]{:S(2)}) copy-start(bf16[2,1664,1536]{2,1,0:T(8,128)(2,1)} %get-tuple-element.19) | copy-start | bytes 30670852
  233.4 9.8 %copy-start.10 = (bf16[2,1664,768]{2,1,0:T(8,128)(2,1)S(1)}, bf16[2,1664,768]{2,1,0:T(8,128)(2,1)}, u32[]{:S(2)}) copy-start(bf16[2,1664,768]{2,1,0:T(8,128)(2,1)} %get-tuple-element.18) | copy-start | bytes 15335428
  243.2 5.7 %copy-start.5 = (bf16[1,2,128,768]{3,2,1,0:T(8,128)(2,1)S(1)}, bf16[1,2,128,768]{3,2,1,0:T(8,128)(2,1)}, u32[]{:S(2)}) copy-start(bf16[1,2,128,768]{3,2,1,0:T(8,128)(2,1)} %param.10) | copy-start | bytes 1179652
  243.2 5.7 %copy-start.8 = (bf16[2,128,768]{2,1,0:T(8,128)(2,1)S(1)}, bf16[2,128,768]{2,1,0:T(8,128)(2,1)}, u32[]{:S(2)}) copy-start(bf16[2,128,768]{2,1,0:T(8,128)(2,1)} %get-tuple-element.17) | copy-start | bytes 1179652
  248.9 1.9 copy-start.6
  248.9 1.9 copy-start.7
  339.9 4.5 copy-start
  479.1 2.2 copy-start.4
  481.3 2.5 copy-start.3
  483.9 2.5 copy-start.2
Sparse Core Ops, SparseCore 0:
  252.9 223.1 all-reduce.2

commit v4 on v3

--- a/solution.py
+++ b/solution.py
@@ -42,7 +42,8 @@
 
 def spread(past, table):
     blocks, rows, width = past.shape
-    chunk = blocks // 2
+    parts = 4
+    chunk = blocks // parts
     cap = 8
 
     def kernel(
@@ -77,7 +78,9 @@
                 device_id=(dp, y * 8 + (1 - x) * 4 + z), device_id_type=MESH,
             )
 
-        ways = ((1, 0, 0), (3, 0, 1), (1, 0, 1), (3, 0, 0), (1, 3, 0), (3, 1, 1))
+        turn = (0, 2, 1, 3)
+        ways = [(way, 0, c) for c in turn for way in ((1, 3) if c < 2 else (3, 1))]
+        ways += [(1, 3, c) if c < 2 else (3, 1, c) for c in turn]
 
         def go(t, n):
             way, owner, c = ways[n]
@@ -124,38 +127,39 @@
                 else:
                     keep(t).start()
 
-        cross(0).start()
-        cross(1).start()
+        for c in turn:
+            cross(c).start()
         local.wait()
-        for n in range(4):
+        for n in range(2 * parts):
             go(0, n).start()
-        crossed(0).wait_recv()
-        go(1, 0).start()
-        go(1, 3).start()
-        came(0, 0).wait_recv()
-        go(0, 4).start()
-        came(0, 1).wait_recv()
-        go(0, 5).start()
-        crossed(1).wait_recv()
-        go(1, 1).start()
-        go(1, 2).start()
-        for n in (2, 3, 4, 5):
-            came(0, n).wait_recv()
-        came(1, 0).wait_recv()
-        go(1, 4).start()
-        came(1, 1).wait_recv()
-        go(1, 5).start()
-        for n in (2, 3, 4, 5):
-            came(1, n).wait_recv()
+
+        def relay(t, i):
+            came(t, 2 * i).wait_recv()
+            go(t, 2 * parts + i).start()
+
+        for i in range(parts):
+            crossed(turn[i]).wait_recv()
+            go(1, 2 * i).start()
+            go(1, 2 * i + 1).start()
+            relay(0, i)
+        for i in range(parts):
+            relay(1, i)
+        for t in (0, 1):
+            for n in range(2 * parts):
+                if n % 2:
+                    came(t, n).wait_recv()
+            for n in range(2 * parts, 3 * parts):
+                came(t, n).wait_recv()
         choose(0)
         choose(1)
         for t in (0, 1):
             for hop in (1, 2, 3):
                 swap(t, hop, True).wait_recv()
             keep(t).wait()
+        for c in turn:
+            cross(c).wait_send()
         for t in (0, 1):
-            cross(t).wait_send()
-            for n in range(6):
+            for n in range(3 * parts):
                 go(t, n).wait_send()
             for hop in (1, 2, 3):
                 swap(t, hop).wait_send()
@@ -171,10 +175,10 @@
             pltpu.VMEM((4, cap, rows, width), past.dtype),
             pltpu.VMEM((4, cap, rows, width), past.dtype),
             pltpu.SemaphoreType.DMA,
-            pltpu.SemaphoreType.DMA((2,)),
-            pltpu.SemaphoreType.DMA((2,)),
-            pltpu.SemaphoreType.DMA((2, 6)),
-            pltpu.SemaphoreType.DMA((2, 6)),
+            pltpu.SemaphoreType.DMA((parts,)),
+            pltpu.SemaphoreType.DMA((parts,)),
+            pltpu.SemaphoreType.DMA((2, 3 * parts)),
+            pltpu.SemaphoreType.DMA((2, 3 * parts)),
             pltpu.SemaphoreType.DMA((2, 3)),
             pltpu.SemaphoreType.DMA((2, 3)),
             pltpu.SemaphoreType.DMA((2,)),
@@ -363,6 +367,195 @@
         ),
         name="collect",
     )(partial)
+
+
+def reduce_weights(grads):
+    rows, width = grads[0].shape
+    block = rows // 24
+    half = 48
+
+    def kernel(
+        a_ref, b_ref, c_ref, d_ref, out_ref, acc, stage, peer, mid, in_a, mid_b, in_b, in_c, got_b, full,
+        core_send, core_recv, send, recv, back_send, back_recv, out_sem,
+    ):
+        y, x_low, z, dp = place()
+        core = dp % 2
+        spot = {"x": (dp // 2) * 2 + x_low, "y": y, "z": z}
+        orders = ("xyz", "yzx", "zxy")
+
+        def there(axis, hop):
+            at = dict(spot)
+            at[axis] = (at[axis] + hop) % 4
+            return (
+                (at["x"] // 2) * 2 + core,
+                at["y"] * 8 + (at["x"] % 2) * 4 + at["z"],
+            )
+
+        other = (dp + 1 - 2 * core, y * 8 + x_low * 4 + z)
+        barrier = pltpu.get_barrier_semaphore()
+        for axis in "xyz":
+            for hop in (1, 2, 3):
+                pl.semaphore_signal(barrier, 1, device_id=there(axis, hop), device_id_type=MESH)
+        pl.semaphore_signal(barrier, 1, device_id=other, device_id_type=MESH)
+
+        def take(keep, give):
+            for i in (0, 1):
+                @pl.loop(0, half // 2)
+                def _(n):
+                    at = pl.ds(pl.multiple_of(n * block, block), block)
+                    stage[i * (half // 2) + n] = give[i][at].astype(BF16)
+                    acc[i * (half // 2) + n] = keep[i][at]
+
+        @pl.when(core == 0)
+        def _():
+            take((a_ref, b_ref), (c_ref, d_ref))
+
+        @pl.when(core == 1)
+        def _():
+            take((c_ref, d_ref), (a_ref, b_ref))
+
+        pl.semaphore_wait(barrier, 10)
+
+        def pair(p):
+            at = pl.ds(p * 16, 16)
+            return pltpu.make_async_remote_copy(
+                stage.at[at], peer.at[at], core_send.at[p], core_recv.at[p],
+                device_id=other, device_id_type=MESH,
+            )
+
+        def copy(source, target, phase, p, hop, sems=None):
+            s, r = sems or (send, recv)
+            return pltpu.make_async_remote_copy(
+                source, target, s.at[phase, p, hop - 1], r.at[phase, p, hop - 1],
+                device_id=there(orders[p][(0, 1, 2, 1, 0)[phase]], hop), device_id_type=MESH,
+            )
+
+        def at_axis(p, phase, hop=0):
+            return (spot[orders[p][phase]] + hop) % 4
+
+        def scatter_a(p, hop):
+            at = pl.ds(p * 16 + at_axis(p, 0, hop) * 4, 4)
+            return copy(mid.at[at], in_a.at[p, hop - 1], 0, p, hop)
+
+        def scatter_b(p, hop):
+            return copy(mid_b.at[p, at_axis(p, 1, hop)], in_b.at[p, hop - 1], 1, p, hop)
+
+        def swap_c(p, hop, arriving=False):
+            to = at_axis(p, 2, -hop if arriving else 0)
+            return copy(in_c.at[p, at_axis(p, 2)], in_c.at[p, to], 2, p, hop)
+
+        def spread_b(p, hop, arriving=False):
+            to = at_axis(p, 1, -hop if arriving else 0)
+            return copy(got_b.at[p, at_axis(p, 1)], got_b.at[p, to], 3, p, hop)
+
+        def spread_a(p, hop, arriving=False):
+            row = lambda back: pl.ds(core * half + p * 16 + at_axis(p, 0, back) * 4, 4)
+            return copy(
+                full.at[row(0)], full.at[row(-hop if arriving else 0)], 4, p, hop
+            )
+
+        def final(p, arriving=False):
+            side = 1 - core if arriving else core
+            at = pl.ds(side * half + p * 16, 16)
+            return pltpu.make_async_remote_copy(
+                full.at[at], full.at[at], back_send.at[p], back_recv.at[p],
+                device_id=other, device_id_type=MESH,
+            )
+
+        hops = (2, 1, 3)
+        for p in range(3):
+            pair(p).start()
+        for p in range(3):
+            pair(p).wait_recv()
+
+            @pl.loop(0, 16)
+            def _(n):
+                total = acc[p * 16 + n] + peer[p * 16 + n].astype(F32)
+                acc[p * 16 + n] = total
+                mid[p * 16 + n] = total.astype(BF16)
+
+            for hop in hops:
+                scatter_a(p, hop).start()
+        for p in range(3):
+            for hop in hops:
+                scatter_a(p, hop).wait_recv()
+
+            @pl.loop(0, 4)
+            def _(n):
+                at = p * 16 + at_axis(p, 0) * 4 + n
+                total = acc[at]
+                for i in range(3):
+                    total = total + in_a[p, i, n].astype(F32)
+                acc[at] = total
+                mid_b[p, n] = total.astype(BF16)
+
+            for hop in hops:
+                scatter_b(p, hop).start()
+        for p in range(3):
+            for hop in hops:
+                scatter_b(p, hop).wait_recv()
+            total = acc[p * 16 + at_axis(p, 0) * 4 + at_axis(p, 1)]
+            for i in range(3):
+                total = total + in_b[p, i].astype(F32)
+            in_c[p, at_axis(p, 2)] = total.astype(BF16)
+            for hop in hops:
+                swap_c(p, hop).start()
+        for p in range(3):
+            for hop in hops:
+                swap_c(p, hop, True).wait_recv()
+            total = in_c[p, 0].astype(F32)
+            for i in range(1, 4):
+                total = total + in_c[p, i].astype(F32)
+            got_b[p, at_axis(p, 1)] = total.astype(BF16)
+            for hop in hops:
+                spread_b(p, hop).start()
+        for p in range(3):
+            for hop in hops:
+                spread_b(p, hop, True).wait_recv()
+
+            @pl.loop(0, 4)
+            def _(n):
+                full[core * half + p * 16 + at_axis(p, 0) * 4 + n] = got_b[p, n]
+
+            for hop in hops:
+                spread_a(p, hop).start()
+        for p in range(3):
+            for hop in hops:
+                spread_a(p, hop, True).wait_recv()
+            final(p).start()
+        for p in range(3):
+            final(p, True).wait_recv()
+        done = pltpu.make_async_copy(full, out_ref, out_sem)
+        done.start()
+        for p in range(3):
+            pair(p).wait_send()
+            final(p).wait_send()
+            for hop in hops:
+                scatter_a(p, hop).wait_send()
+                scatter_b(p, hop).wait_send()
+                swap_c(p, hop).wait_send()
+                spread_b(p, hop).wait_send()
+                spread_a(p, hop).wait_send()
+        done.wait()
+
+    bf = lambda *s: pltpu.VMEM(s + (block, width), BF16)
+    dma = lambda *s: pltpu.SemaphoreType.DMA(s)
+    out = pl.pallas_call(
+        kernel,
+        out_shape=jax.ShapeDtypeStruct((2 * half, block, width), BF16),
+        in_specs=[pl.BlockSpec(memory_space=pltpu.VMEM)] * 4,
+        out_specs=pl.BlockSpec(memory_space=pl.ANY),
+        scratch_shapes=[
+            pltpu.VMEM((half, block, width), F32),
+            bf(half), bf(half), bf(half), bf(3, 3, 4), bf(3, 4), bf(3, 3), bf(3, 4), bf(3, 4), bf(2 * half),
+            dma(3), dma(3), dma(5, 3, 3), dma(5, 3, 3), dma(3), dma(3), pltpu.SemaphoreType.DMA,
+        ],
+        compiler_params=pltpu.CompilerParams(
+            collective_id=3, has_side_effects=True, vmem_limit_bytes=48 << 20
+        ),
+        name="reduce_weights",
+    )(*grads)
+    return out.reshape(4, rows, width)
 
 
 def scatter_sum(source, target, used, outputs):
@@ -617,17 +810,15 @@
     grad_wv = outer_sum(seen, dkv[:, width:]) * scale
     grad_wq = outer_sum(flat(tokens), flat(dq)) * scale
     grad_wo = outer_sum(flat(mixed), flat(grads)) * scale
-    grad_wq, grad_wk, grad_wv, grad_wo = lax.psum(
-        (grad_wq, grad_wk, grad_wv, grad_wo), ("dp", "patch")
-    )
+    weights = reduce_weights((grad_wq, grad_wk, grad_wv, grad_wo)).astype(F32)
     return (
         attn[None],
         token_grad[None],
         past_grad[None],
-        grad_wq,
-        grad_wk,
-        grad_wv,
-        grad_wo,
+        weights[0],
+        weights[1],
+        weights[2],
+        weights[3],
     )
 
 

time: 495 us -> 486 us (0.982)
  between operations: 14.3 us -> 0.87 us
  Pallas kernels: 429 us -> 440 us
  waiting for transfers between devices: 7.66 us -> 0 us
    pallas_call x0 -> x1, Pallas kernels: none -> 50.3 us  [reduce_weights(): pl.pallas_call(kernel, out_shape=jax.ShapeDtypeStruct((2 * half, block, w...]
    pallas_call x1, Pallas kernels: 109 us -> 93.1 us  [collect(): pl.pallas_call(kernel, out_shape=jax.ShapeDtypeStruct((blocks, rows, widt...]
    pallas_call x1, Pallas kernels: 86.8 us -> 71.4 us  [send_back(): pl.pallas_call(kernel, out_shape=jax.ShapeDtypeStruct(grads.shape, grads....]
    unnamed x30 -> x14, local copies, waits for them, and re-layouts: 18.7 us -> 8.16 us
    pallas_call x1, Pallas kernels: 147 us -> 139 us  [spread(): pl.pallas_call(kernel, out_shape=jax.ShapeDtypeStruct((8 * cap, rows, wid...]
    psum x1 -> x0, waiting for transfers between devices: 7.64 us -> none  [body(): lax.psum((grad_wq, grad_wk, grad_wv, grad_wo), ('dp', 'patch'))]
    slice x0 -> x1, local copies, waits for them, and re-layouts: none -> 6.52 us  [body(): weights[3]]
  transfers between devices with their start and end apart: 1 -> 0, of which waited for: 1 -> 0; matrix products, arithmetic and copies ran while one was open for 0% -> 0% of each run, Pallas kernels for 43% -> 0%
where the time goes in v4:
time: 486 us; the launch traced here: 485 us
  Pallas kernels  440 us (91%)
  matrix products  22.3 us (5%)
  local copies, waits for them, and re-layouts  18 us (4%)
    pallas_call x1, Pallas kernels, spread(): pl.pallas_call(kernel, out_shape=jax.ShapeDtypeStruct((8 * cap, rows, wid...  139 us
    pallas_call x1, Pallas kernels, collect(): pl.pallas_call(kernel, out_shape=jax.ShapeDtypeStruct((blocks, rows, widt...  93.1 us
    pallas_call x1, Pallas kernels, send_back(): pl.pallas_call(kernel, out_shape=jax.ShapeDtypeStruct(grads.shape, grads....  71.4 us
    pallas_call x1, Pallas kernels, layer(): pl.pallas_call(kernel, out_shape=(shape(patches, block, width), shape(pat...  70.8 us
    pallas_call x1, Pallas kernels, reduce_weights(): pl.pallas_call(kernel, out_shape=jax.ShapeDtypeStruct((2 * half, block, w...  50.3 us
    dot_general x4, matrix products, outer_sum(): return lax.dot_general(left, right, TN, preferred_element_type=F32)  22.3 us
    pallas_call x1, Pallas kernels, scatter_sum(): pl.pallas_call(kernel, out_shape=jax.ShapeDtypeStruct((outputs, rows, wid...  15 us

profile of v4, /device:TPU:1, one launch (start us, length us, event | category | flops | bytes accessed | tf_op | source)
XLA Modules:
  0.0 485.4 jit_solution(6096820942697676821)
XLA Ops:
  0.7 0.1 add.148
  0.8 0.1 add.149
  0.9 0.8 copy.22
  1.7 0.1 reshape.515
  1.8 0.8 copy.24
  2.7 0.1 reshape.517
  2.9 0.1 broadcast_compare_fusion
  3.0 0.3 convert_reduce_fusion
  3.2 0.5 fusion.18.position_ref
  3.8 0.3 convert_reduce_fusion.1
  4.1 0.1 reshape.519.used_ref
  4.2 0.1 reshape.518.table_ref
  4.3 0.8 copy.23
  5.1 0.1 reshape.516
  5.3 0.5 fusion.17.live_ref
  5.8 3.3 pad_maximum_fusion.wkv_ref
  9.1 0.0 copy-done.1
  9.1 138.9 %spread.1.arrived_ref = bf16[64,128,768]{2,1,0:T(8,128)(2,1)} custom-call(s32[64]{0:T(128)S(1)} %reshape.518.table_ref, bf16[8,128,768]{2,1,0:T(8,128)(2,1)S(1)} %bitcast.36), custom_call_target="tpu_custom_call" | custom-call | tf_op jit(solution)/shard_map/spread/pallas_call | solution.py:167
  148.1 0.0 copy-start.2
  148.1 70.8 %layer.1 = (bf16[2,128,768]{2,1,0:T(8,128)(2,1)}, bf16[2,128,768]{2,1,0:T(8,128)(2,1)}, bf16[64,128,768]{2,1,0:T(8,128)(2,1)}, bf16[2,1664,768]{2,1,0:T(8,128)(2...) custom-call(s32[24]{0:T(128)} %fusion.18.position_ref, ...), custom_call_target="tpu_custom_call" | custom-call | tf_op jit(solution)/shard_map/layer/pallas_call | solution.py:725
  218.9 2.9 multiply_bitcast_fusion
  221.8 2.0 copy.25.a_ref
  223.8 9.6 %fusion.7.c_ref = f32[768,768]{1,0:T(8,128)} fusion(bf16[3328,768]{1,0:T(8,128)(2,1)} %bitcast.53, bf16[3328,1536]{1,0:T(8,128)(2,1)} %bitcast.51), kind=kOutput, calls=%fused_computation.7 | convolution fusion | flops 3926458368 | bytes 12582912 | tf_op jit(solution)/shard_map/dot_general | solution.py:767
  233.5 7.9 %fusion.4.b_ref = f32[768,768]{1,0:T(8,128)S(1)} fusion(bf16[3328,768]{1,0:T(8,128)(2,1)} %bitcast.54, bf16[3328,1536]{1,0:T(8,128)(2,1)} %bitcast.52), kind=kOutput, calls=%fused_computation.6 | convolution fusion | flops 3926458368 | bytes 12582912 | tf_op jit(solution)/shard_map/dot_general | solution.py:767
  241.4 1.9 convolution_multiply_fusion.d_ref
  243.3 50.3 %reduce_weights.1 = bf16[96,32,768]{2,1,0:T(8,128)(2,1)} custom-call(f32[768,768]{1,0:T(8,128)S(1)} %copy.25.a_ref, f32[768,768]{1,0:T(8,128)S(1)} %fusion.4.b_ref, f32[768,768]{1,0:T(8,128)} %fusion.7.c_ref, f32[768,768]{1,0:T(8,128)} %convolution_multiply_fusion.d_ref), custom_call_target="tpu_custom_call" | custom-call | tf_op jit(solution)/shard_map/reduce_weights/pallas_call | solution.py:543
  293.6 6.5 %fusion.19 = (f32[24,32,768]{2,1,0:T(8,128)}, f32[24,32,768]{2,1,0:T(8,128)}, f32[24,32,768]{2,1,0:T(8,128)}, f32[24,32,768]{2,1,0:T(8,128)}) fusion(bf16[96,32,768]{2,1,0:T(8,128)(2,1)} %reduce_weights.1), kind=kLoop, calls=%fused_computation.49 | loop fusion | bytes 18874368 | tf_op jit(solution)/shard_map/slice | solution.py:821
  300.1 71.4 %send_back.1.source_ref = bf16[64,128,768]{2,1,0:T(8,128)(2,1)S(1)} custom-call(bf16[64,128,768]{2,1,0:T(8,128)(2,1)} %get-tuple-element.16.grad_ref), custom_call_target="tpu_custom_call" | custom-call | tf_op jit(solution)/shard_map/send_back/pallas_call | solution.py:237
  371.6 4.5 copy-done
  376.1 15.0 %scatter_sum.1 = bf16[64,128,768]{2,1,0:T(8,128)(2,1)} custom-call(s32[64]{0:T(128)S(1)} %add.150.target_ref, s32[64]{0:T(128)S(1)} %reshape.519.used_ref, bf16[64,128,768]{2,1,0:T(8,128)(2,1)} %copy-done), custom_call_target="tpu_custom_call" | custom-call | tf_op jit(solution)/shard_map/scatter_sum/pallas_call | solution.py:582
  391.1 93.1 %collect.1 = bf16[8,128,768]{2,1,0:T(8,128)(2,1)S(1)} custom-call(bf16[8,8,128,768]{3,2,1,0:T(8,128)(2,1)} %bitcast.37), custom_call_target="tpu_custom_call" | custom-call | tf_op jit(solution)/shard_map/collect/pallas_call | solution.py:351
  484.2 1.1 copy.27
  (14 shorter events, 0.1 us)
Async XLA Ops:
  5.8 3.3 copy-start.1
  148.1 70.8 %copy-start.2 = (bf16[1,2,128,768]{3,2,1,0:T(8,128)(2,1)S(1)}, bf16[1,2,128,768]{3,2,1,0:T(8,128)(2,1)}, u32[]{:S(2)}) copy-start(bf16[1,2,128,768]{3,2,1,0:T(8,128)(2,1)} %param.10) | copy-start | bytes 1179652
  233.5 7.9 %copy-start.3 = (bf16[1,2,128,768]{3,2,1,0:T(8,128)(2,1)S(1)}, bf16[1,2,128,768]{3,2,1,0:T(8,128)(2,1)}, u32[]{:S(2)}) copy-start(bf16[1,2,128,768]{3,2,1,0:T(8,128)(2,1)} %param.19) | copy-start | bytes 1179652
  233.5 7.9 %copy-start.4 = (bf16[2,128,768]{2,1,0:T(8,128)(2,1)S(1)}, bf16[2,128,768]{2,1,0:T(8,128)(2,1)}, u32[]{:S(2)}) copy-start(bf16[2,128,768]{2,1,0:T(8,128)(2,1)} %get-tuple-element.20) | copy-start | bytes 1179652
  371.6 4.6 copy-start

commit v5 on v4

--- a/solution.py
+++ b/solution.py
@@ -190,11 +190,16 @@
     )(table, past)
 
 
-def send_back(grads):
+def send_back(grads, tokens, grad_out, seen, dkv, dq, mixed):
     slots, rows, width = grads.shape
     cap = slots // 8
-
-    def kernel(grad_ref, out_ref, own, send, recv, own_sem):
+    total = seen.shape[0]
+    chunk = total // 8
+
+    def kernel(
+        grad_ref, tok_ref, gout_ref, seen_ref, dkv_ref, dq_ref, mixed_ref,
+        out_ref, wq_ref, wk_ref, wv_ref, wo_ref, own, send, recv, own_sem,
+    ):
         y, x, z, dp = place()
         pos = lambda dim, hop=0: (y * (1 - dim) + z * dim + hop) % 4
         part = lambda ref, at: ref.at[pl.ds(at * cap, cap)]
@@ -226,6 +231,18 @@
         for h in (0, 1):
             load(h).wait()
             store(h).start()
+        wq_ref[...] = mm(tok_ref[...], dq_ref[...], TN)
+        wo_ref[...] = mm(mixed_ref[...], gout_ref[...], TN)
+        wk_ref[...] = jnp.zeros_like(wk_ref)
+        wv_ref[...] = jnp.zeros_like(wv_ref)
+
+        @pl.loop(0, total // chunk)
+        def _(n):
+            at = pl.ds(pl.multiple_of(n * chunk, 16), chunk)
+            left = seen_ref[at]
+            wk_ref[...] += mm(left, dkv_ref[at, :width], TN)
+            wv_ref[...] += mm(left, dkv_ref[at, width:], TN)
+
         for h in (0, 1):
             store(h).wait()
             for hop in (1, 2, 3):
@@ -236,9 +253,10 @@
 
     return pl.pallas_call(
         kernel,
-        out_shape=jax.ShapeDtypeStruct(grads.shape, grads.dtype),
-        in_specs=[pl.BlockSpec(memory_space=pl.ANY)],
-        out_specs=pl.BlockSpec(memory_space=pl.ANY),
+        out_shape=(jax.ShapeDtypeStruct(grads.shape, grads.dtype),)
+        + (jax.ShapeDtypeStruct((width, width), F32),) * 4,
+        in_specs=[pl.BlockSpec(memory_space=pl.ANY)] + [pl.BlockSpec(memory_space=pltpu.VMEM)] * 6,
+        out_specs=(pl.BlockSpec(memory_space=pl.ANY),) + (pl.BlockSpec(memory_space=pltpu.VMEM),) * 4,
         scratch_shapes=[
             pltpu.VMEM((2, cap, rows, width), grads.dtype),
             pltpu.SemaphoreType.DMA((2, 3)),
@@ -246,24 +264,26 @@
             pltpu.SemaphoreType.DMA((2,)),
         ],
         compiler_params=pltpu.CompilerParams(
-            collective_id=1, has_side_effects=True, vmem_limit_bytes=32 << 20
+            collective_id=1, has_side_effects=True, vmem_limit_bytes=56 << 20
         ),
         name="send_back",
-    )(grads)
-
-
-def collect(partial):
+    )(grads, tokens, grad_out, seen, dkv, dq, mixed)
+
+
+def collect(partial, grads, scale):
     groups, blocks, rows, width = partial.shape
     chunk = blocks // 2
-
-    def kernel(
+    w_rows = grads[0].shape[0]
+    block = w_rows // 24
+    half_w = 48
+
+    def collect_steps(
         part_ref, out_ref, relay, staged, inward, mine, across,
         r_send, r_recv, d_send, d_recv, x_send, x_recv,
     ):
         y, x, z, dp = place()
         pos = lambda dim, hop=0: (y * (1 - dim) + z * dim + hop) % 4
         half = (1 - x, x)
-        meet(y, x, z, dp, True)
         ways = (3, 1)
 
         def row(t, hop):
@@ -308,6 +328,7 @@
         for t in (0, 1):
             for side in (0, 1):
                 direct(t, side, False).start()
+        yield
         for t in (0, 1):
             for side in (0, 1):
                 pass_on(t, side).wait_recv()
@@ -320,6 +341,7 @@
                     ).astype(staged.dtype)
 
                 direct(t, side, True).start()
+        yield
         for side in (0, 1):
             for summed in (False, True):
                 direct(0, side, summed).wait_recv()
@@ -329,6 +351,7 @@
                 mine[c * chunk + b] = final(0, c * chunk + b).astype(mine.dtype)
 
             cross(c).start()
+        yield
         for side in (0, 1):
             for summed in (False, True):
                 direct(1, side, summed).wait_recv()
@@ -340,6 +363,7 @@
                 at = c * chunk + b
                 out_ref[at] = (final(1, at) + across[at].astype(F32)).astype(out_ref.dtype)
 
+        yield
         for t in (0, 1):
             cross(t).wait_send()
             for side in (0, 1):
@@ -347,34 +371,7 @@
                 for summed in (False, True):
                     direct(t, side, summed).wait_send()
 
-    shape = lambda *s: pltpu.VMEM(s + (rows, width), partial.dtype)
-    return pl.pallas_call(
-        kernel,
-        out_shape=jax.ShapeDtypeStruct((blocks, rows, width), partial.dtype),
-        in_specs=[pl.BlockSpec(memory_space=pltpu.VMEM)],
-        out_specs=pl.BlockSpec(memory_space=pltpu.VMEM),
-        scratch_shapes=[
-            shape(2, 2, chunk), shape(2, 2, chunk), shape(2, 2, blocks), shape(blocks), shape(blocks),
-            pltpu.SemaphoreType.DMA((2, 2)),
-            pltpu.SemaphoreType.DMA((2, 2)),
-            pltpu.SemaphoreType.DMA((2, 2, 2)),
-            pltpu.SemaphoreType.DMA((2, 2, 2)),
-            pltpu.SemaphoreType.DMA((2,)),
-            pltpu.SemaphoreType.DMA((2,)),
-        ],
-        compiler_params=pltpu.CompilerParams(
-            collective_id=2, has_side_effects=True, vmem_limit_bytes=48 << 20
-        ),
-        name="collect",
-    )(partial)
-
-
-def reduce_weights(grads):
-    rows, width = grads[0].shape
-    block = rows // 24
-    half = 48
-
-    def kernel(
+    def reduce_steps(
         a_ref, b_ref, c_ref, d_ref, out_ref, acc, stage, peer, mid, in_a, mid_b, in_b, in_c, got_b, full,
         core_send, core_recv, send, recv, back_send, back_recv, out_sem,
     ):
@@ -397,14 +394,16 @@
             for hop in (1, 2, 3):
                 pl.semaphore_signal(barrier, 1, device_id=there(axis, hop), device_id_type=MESH)
         pl.semaphore_signal(barrier, 1, device_id=other, device_id_type=MESH)
+        pl.semaphore_wait(barrier, 10)
+        yield
 
         def take(keep, give):
             for i in (0, 1):
-                @pl.loop(0, half // 2)
+                @pl.loop(0, half_w // 2)
                 def _(n):
                     at = pl.ds(pl.multiple_of(n * block, block), block)
-                    stage[i * (half // 2) + n] = give[i][at].astype(BF16)
-                    acc[i * (half // 2) + n] = keep[i][at]
+                    stage[i * (half_w // 2) + n] = (give[i][at] * scale).astype(BF16)
+                    acc[i * (half_w // 2) + n] = keep[i][at] * scale
 
         @pl.when(core == 0)
         def _():
@@ -414,8 +413,6 @@
         def _():
             take((c_ref, d_ref), (a_ref, b_ref))
 
-        pl.semaphore_wait(barrier, 10)
-
         def pair(p):
             at = pl.ds(p * 16, 16)
             return pltpu.make_async_remote_copy(
@@ -449,14 +446,14 @@
             return copy(got_b.at[p, at_axis(p, 1)], got_b.at[p, to], 3, p, hop)
 
         def spread_a(p, hop, arriving=False):
-            row = lambda back: pl.ds(core * half + p * 16 + at_axis(p, 0, back) * 4, 4)
+            row = lambda back: pl.ds(core * half_w + p * 16 + at_axis(p, 0, back) * 4, 4)
             return copy(
                 full.at[row(0)], full.at[row(-hop if arriving else 0)], 4, p, hop
             )
 
         def final(p, arriving=False):
             side = 1 - core if arriving else core
-            at = pl.ds(side * half + p * 16, 16)
+            at = pl.ds(side * half_w + p * 16, 16)
             return pltpu.make_async_remote_copy(
                 full.at[at], full.at[at], back_send.at[p], back_recv.at[p],
                 device_id=other, device_id_type=MESH,
@@ -465,6 +462,7 @@
         hops = (2, 1, 3)
         for p in range(3):
             pair(p).start()
+        yield
         for p in range(3):
             pair(p).wait_recv()
 
@@ -476,6 +474,7 @@
 
             for hop in hops:
                 scatter_a(p, hop).start()
+        yield
         for p in range(3):
             for hop in hops:
                 scatter_a(p, hop).wait_recv()
@@ -491,6 +490,7 @@
 
             for hop in hops:
                 scatter_b(p, hop).start()
+        yield
         for p in range(3):
             for hop in hops:
                 scatter_b(p, hop).wait_recv()
@@ -500,6 +500,7 @@
             in_c[p, at_axis(p, 2)] = total.astype(BF16)
             for hop in hops:
                 swap_c(p, hop).start()
+        yield
         for p in range(3):
             for hop in hops:
                 swap_c(p, hop, True).wait_recv()
@@ -509,24 +510,28 @@
             got_b[p, at_axis(p, 1)] = total.astype(BF16)
             for hop in hops:
                 spread_b(p, hop).start()
+        yield
         for p in range(3):
             for hop in hops:
                 spread_b(p, hop, True).wait_recv()
 
             @pl.loop(0, 4)
             def _(n):
-                full[core * half + p * 16 + at_axis(p, 0) * 4 + n] = got_b[p, n]
+                full[core * half_w + p * 16 + at_axis(p, 0) * 4 + n] = got_b[p, n]
 
             for hop in hops:
                 spread_a(p, hop).start()
+        yield
         for p in range(3):
             for hop in hops:
                 spread_a(p, hop, True).wait_recv()
             final(p).start()
+        yield
         for p in range(3):
             final(p, True).wait_recv()
         done = pltpu.make_async_copy(full, out_ref, out_sem)
         done.start()
+        yield
         for p in range(3):
             pair(p).wait_send()
             final(p).wait_send()
@@ -538,24 +543,38 @@
                 spread_a(p, hop).wait_send()
         done.wait()
 
+    def kernel(part_ref, a, b, c, d, out_ref, weights_ref, *scratch):
+        weights = reduce_steps(a, b, c, d, weights_ref, *scratch[11:])
+        blocks_back = collect_steps(part_ref, out_ref, *scratch[:11])
+        for step in "wbwwbwwbwwwbwbw":
+            next(weights if step == "w" else blocks_back, None)
+
+    shape = lambda *s: pltpu.VMEM(s + (rows, width), partial.dtype)
     bf = lambda *s: pltpu.VMEM(s + (block, width), BF16)
     dma = lambda *s: pltpu.SemaphoreType.DMA(s)
-    out = pl.pallas_call(
+    vmem = pl.BlockSpec(memory_space=pltpu.VMEM)
+    past_grad, weights = pl.pallas_call(
         kernel,
-        out_shape=jax.ShapeDtypeStruct((2 * half, block, width), BF16),
-        in_specs=[pl.BlockSpec(memory_space=pltpu.VMEM)] * 4,
-        out_specs=pl.BlockSpec(memory_space=pl.ANY),
+        out_shape=(
+            jax.ShapeDtypeStruct((blocks, rows, width), partial.dtype),
+            jax.ShapeDtypeStruct((2 * half_w, block, width), BF16),
+        ),
+        in_specs=[vmem] * 5,
+        out_specs=(vmem, pl.BlockSpec(memory_space=pl.ANY)),
         scratch_shapes=[
-            pltpu.VMEM((half, block, width), F32),
-            bf(half), bf(half), bf(half), bf(3, 3, 4), bf(3, 4), bf(3, 3), bf(3, 4), bf(3, 4), bf(2 * half),
+            shape(2, 2, chunk), shape(2, 2, chunk), shape(2, 2, blocks), shape(blocks), shape(blocks),
+            dma(2, 2), dma(2, 2), dma(2, 2, 2), dma(2, 2, 2), dma(2), dma(2),
+            pltpu.VMEM((half_w, block, width), F32),
+            bf(half_w), bf(half_w), bf(half_w), bf(3, 3, 4), bf(3, 4), bf(3, 3), bf(3, 4), bf(3, 4),
+            bf(2 * half_w),
             dma(3), dma(3), dma(5, 3, 3), dma(5, 3, 3), dma(3), dma(3), pltpu.SemaphoreType.DMA,
         ],
         compiler_params=pltpu.CompilerParams(
-            collective_id=3, has_side_effects=True, vmem_limit_bytes=48 << 20
+            collective_id=2, has_side_effects=True, vmem_limit_bytes=62 << 20
         ),
-        name="reduce_weights",
-    )(*grads)
-    return out.reshape(4, rows, width)
+        name="collect",
+    )(partial, *grads)
+    return past_grad, weights.reshape(4, w_rows, width)
 
 
 def scatter_sum(source, target, used, outputs):
@@ -763,10 +782,6 @@
     )(position, live, arrived, tokens, grad_out, w_query, w_pair, w_out)
 
 
-def outer_sum(left, right):
-    return lax.dot_general(left, right, TN, preferred_element_type=F32)
-
-
 def body(
     query_tokens, past_tokens, source_dev, source_slot, kept, w_query, w_key, w_value, w_out,
     grad_out,
@@ -800,17 +815,14 @@
     attn, token_grad, far_grad, seen, dkv, dq, mixed = layer(
         mine, live, arrived, tokens, grads, w_query, w_pair, w_out, 8 * cap
     )
-    returned = send_back(far_grad)
+    flat = lambda a: a.reshape(-1, a.shape[-1])
+    returned, *weight_grads = send_back(
+        far_grad, flat(tokens), flat(grads), flat(seen), flat(dkv), flat(dq), flat(mixed)
+    )
     partial = scatter_sum(returned, target, used, 8 * past.shape[0])
-    past_grad = collect(partial.reshape((8,) + past.shape))
-    flat = lambda a: a.reshape(-1, a.shape[-1])
     scale = 1.0 / math.sqrt(lax.axis_size("dp") * peers * patches * block)
-    dkv, seen = flat(dkv), flat(seen)
-    grad_wk = outer_sum(seen, dkv[:, :width]) * scale
-    grad_wv = outer_sum(seen, dkv[:, width:]) * scale
-    grad_wq = outer_sum(flat(tokens), flat(dq)) * scale
-    grad_wo = outer_sum(flat(mixed), flat(grads)) * scale
-    weights = reduce_weights((grad_wq, grad_wk, grad_wv, grad_wo)).astype(F32)
+    past_grad, weights = collect(partial.reshape((8,) + past.shape), weight_grads, scale)
+    weights = weights.astype(F32)
     return (
         attn[None],
         token_grad[None],

time: 486 us -> 452 us (0.930)
  matrix products: 22.3 us -> 0 us
  local copies, waits for them, and re-layouts: 18 us -> 11.5 us
  Pallas kernels: 440 us -> 435 us
    dot_general x4 -> x0, matrix products: 22.3 us -> none  [outer_sum(): return lax.dot_general(left, right, TN, preferred_element_type=F32)]
    pallas_call x3 -> x2, Pallas kernels: 215 us -> 210 us  [the longest x1 129 us: collect(): pl.pallas_call(kernel, out_shape=(jax.ShapeDtypeStruct((blocks, rows, wid...]
where the time goes in v5:
time: 452 us
  Pallas kernels  435 us (96%)
  local copies, waits for them, and re-layouts  11.5 us (3%)
  other arithmetic  4.59 us (1%)
    pallas_call x1, Pallas kernels, spread(): pl.pallas_call(kernel, out_shape=jax.ShapeDtypeStruct((8 * cap, rows, wid...  139 us
    pallas_call x1, Pallas kernels, collect(): pl.pallas_call(kernel, out_shape=(jax.ShapeDtypeStruct((blocks, rows, wid...  129 us
    pallas_call x1, Pallas kernels, send_back(): pl.pallas_call(kernel, out_shape=(jax.ShapeDtypeStruct(grads.shape, grads...  81.4 us
    pallas_call x1, Pallas kernels, layer(): pl.pallas_call(kernel, out_shape=(shape(patches, block, width), shape(pat...  70.7 us
    pallas_call x1, Pallas kernels, scatter_sum(): pl.pallas_call(kernel, out_shape=jax.ShapeDtypeStruct((outputs, rows, wid...  15.1 us

profile of v5, /device:TPU:1, one launch (start us, length us, event | category | flops | bytes accessed | tf_op | source)
XLA Modules:
  0.0 451.7 jit_solution(9886095002186539801)
XLA Ops:
  0.7 0.1 add.148
  0.8 0.1 add.149
  0.9 0.8 copy.20
  1.7 0.1 reshape.515
  1.8 0.8 copy.22
  2.7 0.1 reshape.517
  2.9 0.1 broadcast_compare_fusion
  2.9 0.3 convert_reduce_fusion
  3.2 0.5 fusion.8.position_ref
  3.8 0.3 convert_reduce_fusion.1
  4.1 0.1 reshape.519.used_ref
  4.2 0.1 reshape.518.table_ref
  4.3 0.8 copy.21
  5.1 0.1 reshape.516
  5.3 0.5 fusion.7.live_ref
  5.8 0.0 copy-start
  5.8 3.3 pad_maximum_fusion.wkv_ref
  9.1 0.0 copy-done
  9.1 138.9 %spread.1.arrived_ref = bf16[64,128,768]{2,1,0:T(8,128)(2,1)} custom-call(s32[64]{0:T(128)S(1)} %reshape.518.table_ref, bf16[8,128,768]{2,1,0:T(8,128)(2,1)S(1)} %bitcast.27), custom_call_target="tpu_custom_call" | custom-call | tf_op jit(solution)/shard_map/spread/pallas_call | solution.py:167
  148.0 70.7 %layer.1 = (bf16[2,128,768]{2,1,0:T(8,128)(2,1)}, bf16[2,128,768]{2,1,0:T(8,128)(2,1)}, bf16[64,128,768]{2,1,0:T(8,128)(2,1)}, bf16[2,1664,768]{2,1,0:T(8,128)(2...) custom-call(s32[24]{0:T(128)} %fusion.8.position_ref, ...), custom_call_target="tpu_custom_call" | custom-call | tf_op jit(solution)/shard_map/layer/pallas_call | solution.py:744
  218.8 81.4 %send_back.1 = (bf16[64,128,768]{2,1,0:T(8,128)(2,1)}, f32[768,768]{1,0:T(8,128)}, f32[768,768]{1,0:T(8,128)}, f32[768,768]{1,0:T(8,128)}, f32[768,768]{1,0:T(8,128)}) custom-call(bf16[64,128,768]{2,1,0:T(8,128)(2,1)} %get-tuple-element.23.grad_ref, bf16[256,768]{1,0:T(8,128)(2,1)} %bitcast.36, bf16[256,768]{1,0:T(8,128)(2,1)} %bitcast.38, ...), custom_call_target="tpu_custom_call" | custom-call | tf_op jit(solution)/shard_map/send_back/pallas_call | solution.py:254
  300.2 15.1 %scatter_sum.1 = bf16[64,128,768]{2,1,0:T(8,128)(2,1)} custom-call(s32[64]{0:T(128)S(1)} %add.150.target_ref, s32[64]{0:T(128)S(1)} %reshape.519.used_ref, bf16[64,128,768]{2,1,0:T(8,128)(2,1)} %get-tuple-element.28.source_ref), custom_call_target="tpu_custom_call" | custom-call | tf_op jit(solution)/shard_map/scatter_sum/pallas_call | solution.py:601
  315.3 128.6 %collect.1 = (bf16[8,128,768]{2,1,0:T(8,128)(2,1)}, bf16[96,32,768]{2,1,0:T(8,128)(2,1)}) custom-call(bf16[8,8,128,768]{3,2,1,0:T(8,128)(2,1)} %bitcast.28, f32[768,768]{1,0:T(8,128)} %get-tuple-element.29.a, f32[768,768]{1,0:T(8,128)} %get-tuple-element.30.b, f32[768,768]{1,0:T(8,128)} %get-tuple-element.31.c, f32[768,768]{1,0:T(8,128)} %get-tuple-element.32.d), custom_call_target="tpu_custom_call" | custom-call | tf_op jit(solution)/shard_map/collect/pallas_call | solution.py:556
  443.9 0.0 copy-start.1
  443.9 6.6 %fusion.9 = (f32[24,32,768]{2,1,0:T(8,128)}, f32[24,32,768]{2,1,0:T(8,128)}, f32[24,32,768]{2,1,0:T(8,128)}, f32[24,32,768]{2,1,0:T(8,128)}) fusion(bf16[96,32,768]{2,1,0:T(8,128)(2,1)} %get-tuple-element.34), kind=kLoop, calls=%fused_computation.41 | loop fusion | bytes 18874368 | tf_op jit(solution)/shard_map/slice | solution.py:833
  450.5 0.0 copy-done.1
  450.5 1.1 copy.24
  (7 shorter events, 0.1 us)
Async XLA Ops:
  5.8 3.3 copy-start
  443.9 6.6 %copy-start.1 = (bf16[8,128,768]{2,1,0:T(8,128)(2,1)S(1)}, bf16[8,128,768]{2,1,0:T(8,128)(2,1)}, u32[]{:S(2)}) copy-start(bf16[8,128,768]{2,1,0:T(8,128)(2,1)} %get-tuple-element.33) | copy-start | bytes 4718596

commit v6 on v5

--- a/solution.py
+++ b/solution.py
@@ -40,11 +40,11 @@
     pl.semaphore_wait(barrier, len(ids))
 
 
-def spread(past, table):
+def spread(past, table, ident):
     blocks, rows, width = past.shape
     parts = 4
     chunk = blocks // parts
-    cap = 8
+    cap = table.shape[0] // 8
 
     def kernel(
         table_ref, past_ref, out_ref, have_a, have_b, sel_a, sel_b,
@@ -184,22 +184,28 @@
             pltpu.SemaphoreType.DMA((2,)),
         ],
         compiler_params=pltpu.CompilerParams(
-            collective_id=0, has_side_effects=True, vmem_limit_bytes=48 << 20
+            collective_id=ident, has_side_effects=True, vmem_limit_bytes=48 << 20
         ),
         name="spread",
     )(table, past)
 
 
-def send_back(grads, tokens, grad_out, seen, dkv, dq, mixed):
+def send_back(grads, tokens, grad_out, seen, dkv, dq, mixed, ident):
     slots, rows, width = grads.shape
     cap = slots // 8
     total = seen.shape[0]
     chunk = total // 8
 
     def kernel(
-        grad_ref, tok_ref, gout_ref, seen_ref, dkv_ref, dq_ref, mixed_ref,
+        grad_ref, tok_in, gout_in, seen_in, dkv_in, dq_in, mixed_in,
         out_ref, wq_ref, wk_ref, wv_ref, wo_ref, own, send, recv, own_sem,
+        tok_ref, gout_ref, seen_ref, dkv_ref, dq_ref, mixed_ref, op_sem,
     ):
+        pairs = (
+            (tok_in, tok_ref), (dq_in, dq_ref), (mixed_in, mixed_ref), (gout_in, gout_ref),
+            (seen_in, seen_ref), (dkv_in, dkv_ref),
+        )
+        operands = [pltpu.make_async_copy(a, b, op_sem.at[i]) for i, (a, b) in enumerate(pairs)]
         y, x, z, dp = place()
         pos = lambda dim, hop=0: (y * (1 - dim) + z * dim + hop) % 4
         part = lambda ref, at: ref.at[pl.ds(at * cap, cap)]
@@ -231,6 +237,10 @@
         for h in (0, 1):
             load(h).wait()
             store(h).start()
+        for operand in operands:
+            operand.start()
+        for operand in operands:
+            operand.wait()
         wq_ref[...] = mm(tok_ref[...], dq_ref[...], TN)
         wo_ref[...] = mm(mixed_ref[...], gout_ref[...], TN)
         wk_ref[...] = jnp.zeros_like(wk_ref)
@@ -255,16 +265,18 @@
         kernel,
         out_shape=(jax.ShapeDtypeStruct(grads.shape, grads.dtype),)
         + (jax.ShapeDtypeStruct((width, width), F32),) * 4,
-        in_specs=[pl.BlockSpec(memory_space=pl.ANY)] + [pl.BlockSpec(memory_space=pltpu.VMEM)] * 6,
+        in_specs=[pl.BlockSpec(memory_space=pl.ANY)] * 7,
         out_specs=(pl.BlockSpec(memory_space=pl.ANY),) + (pl.BlockSpec(memory_space=pltpu.VMEM),) * 4,
         scratch_shapes=[
             pltpu.VMEM((2, cap, rows, width), grads.dtype),
             pltpu.SemaphoreType.DMA((2, 3)),
             pltpu.SemaphoreType.DMA((2, 3)),
             pltpu.SemaphoreType.DMA((2,)),
-        ],
+        ]
+        + [pltpu.VMEM(a.shape, a.dtype) for a in (tokens, grad_out, seen, dkv, dq, mixed)]
+        + [pltpu.SemaphoreType.DMA((6,))],
         compiler_params=pltpu.CompilerParams(
-            collective_id=1, has_side_effects=True, vmem_limit_bytes=56 << 20
+            collective_id=ident, has_side_effects=True, vmem_limit_bytes=56 << 20
         ),
         name="send_back",
     )(grads, tokens, grad_out, seen, dkv, dq, mixed)
@@ -278,12 +290,14 @@
     half_w = 48
 
     def collect_steps(
-        part_ref, out_ref, relay, staged, inward, mine, across,
+        part_in, part_ref, part_sem, out_ref, relay, staged, inward, mine, across,
         r_send, r_recv, d_send, d_recv, x_send, x_recv,
     ):
         y, x, z, dp = place()
         pos = lambda dim, hop=0: (y * (1 - dim) + z * dim + hop) % 4
         half = (1 - x, x)
+        held = pltpu.make_async_copy(part_in, part_ref, part_sem)
+        held.start()
         ways = (3, 1)
 
         def row(t, hop):
@@ -291,7 +305,7 @@
 
         def pass_on(t, side):
             return pltpu.make_async_remote_copy(
-                part_ref.at[row(t, 2), pl.ds(side * chunk, chunk)], relay.at[t, side],
+                part_in.at[row(t, 2), pl.ds(side * chunk, chunk)], relay.at[t, side],
                 r_send.at[t, side], r_recv.at[t, side],
                 device_id=(dp, step_id(y, x, z, half[t], ways[side])), device_id_type=MESH,
             )
@@ -300,7 +314,7 @@
             c = side if summed else 1 - side
             source = (
                 staged.at[t, side] if summed
-                else part_ref.at[row(t, ways[side]), pl.ds(c * chunk, chunk)]
+                else part_in.at[row(t, ways[side]), pl.ds(c * chunk, chunk)]
             )
             return pltpu.make_async_remote_copy(
                 source, inward.at[t, side, pl.ds(c * chunk, chunk)],
@@ -329,6 +343,7 @@
             for side in (0, 1):
                 direct(t, side, False).start()
         yield
+        held.wait()
         for t in (0, 1):
             for side in (0, 1):
                 pass_on(t, side).wait_recv()
@@ -372,13 +387,17 @@
                     direct(t, side, summed).wait_send()
 
     def reduce_steps(
-        a_ref, b_ref, c_ref, d_ref, out_ref, acc, stage, peer, mid, in_a, mid_b, in_b, in_c, got_b, full,
+        given, refs, grad_sem, out_ref, acc, stage, peer, mid, in_a, mid_b, in_b, in_c, got_b, full,
         core_send, core_recv, send, recv, back_send, back_recv, out_sem,
     ):
         y, x_low, z, dp = place()
         core = dp % 2
         spot = {"x": (dp // 2) * 2 + x_low, "y": y, "z": z}
         orders = ("xyz", "yzx", "zxy")
+        a_ref, b_ref, c_ref, d_ref = refs
+        loads = [pltpu.make_async_copy(given[i], refs[i], grad_sem.at[i]) for i in range(4)]
+        for load in loads:
+            load.start()
 
         def there(axis, hop):
             at = dict(spot)
@@ -396,6 +415,8 @@
         pl.semaphore_signal(barrier, 1, device_id=other, device_id_type=MESH)
         pl.semaphore_wait(barrier, 10)
         yield
+        for load in loads:
+            load.wait()
 
         def take(keep, give):
             for i in (0, 1):
@@ -543,9 +564,11 @@
                 spread_a(p, hop).wait_send()
         done.wait()
 
-    def kernel(part_ref, a, b, c, d, out_ref, weights_ref, *scratch):
-        weights = reduce_steps(a, b, c, d, weights_ref, *scratch[11:])
-        blocks_back = collect_steps(part_ref, out_ref, *scratch[:11])
+    def kernel(part_in, a, b, c, d, out_ref, weights_ref, part_ref, part_sem, *scratch):
+        weights = reduce_steps(
+            (a, b, c, d), scratch[:4], scratch[4], weights_ref, *scratch[16:]
+        )
+        blocks_back = collect_steps(part_in, part_ref, part_sem, out_ref, *scratch[5:16])
         for step in "wbwwbwwbwwwbwbw":
             next(weights if step == "w" else blocks_back, None)
 
@@ -559,9 +582,11 @@
             jax.ShapeDtypeStruct((blocks, rows, width), partial.dtype),
             jax.ShapeDtypeStruct((2 * half_w, block, width), BF16),
         ),
-        in_specs=[vmem] * 5,
+        in_specs=[pl.BlockSpec(memory_space=pl.ANY)] * 5,
         out_specs=(vmem, pl.BlockSpec(memory_space=pl.ANY)),
         scratch_shapes=[
+            shape(groups, blocks), pltpu.SemaphoreType.DMA,
+            *[pltpu.VMEM(a.shape, a.dtype) for a in grads], dma(4),
             shape(2, 2, chunk), shape(2, 2, chunk), shape(2, 2, blocks), shape(blocks), shape(blocks),
             dma(2, 2), dma(2, 2), dma(2, 2, 2), dma(2, 2, 2), dma(2), dma(2),
             pltpu.VMEM((half_w, block, width), F32),
@@ -733,9 +758,14 @@
             )
 
         for r in range(requests):
-            put(r).start()
+            @pl.when(live_ref[p * requests + r] > 0)
+            def _():
+                put(r).start()
+
         for r in range(requests):
-            put(r).wait()
+            @pl.when(live_ref[p * requests + r] > 0)
+            def _():
+                put(r).wait()
 
     per_patch = lambda n, w: pl.BlockSpec((1, n, w), lambda p, *_: (p, 0, 0))
     whole = lambda a: pl.BlockSpec(a.shape, lambda p, *_: (0, 0), pipeline_mode=pl.Buffered(1))
@@ -791,35 +821,44 @@
     peers = lax.axis_size("patch")
     y, x, z, _ = place()
     per_device = patches * source_dev.shape[1] * source_dev.shape[2]
-    cap = 8
+    blocks = past.shape[0]
 
     grid = lambda a: a.reshape(4, 2, 4, per_device)
     near = lambda a: jnp.concatenate([grid(a)[y, x], grid(a)[:, x, z]], axis=0)
-    owner, slot = near(source_dev), near(source_slot)
+    owner, slot, kept = (a.reshape(peers, per_device) for a in (source_dev, source_slot, kept))
     from_y, half, from_z = owner // 8, (owner // 4) % 2, owner % 4
     key = half * 4 + jnp.where(half == 0, from_z, from_y)
-    number = jnp.where(half == 0, from_y, from_z) * past.shape[0] + slot
+    number = jnp.where(half == 0, from_y, from_z) * blocks + slot
+    key = jnp.where(kept > 0, key, 8)
+    most = jnp.max(jnp.sum((key[:, None, :] == jnp.arange(8)[None, :, None]).astype(jnp.int32), axis=2))
+    key, number = near(key), near(number)
     order = jnp.arange(per_device)
     matches = (key[:, :, None] == key[:, None, :]) & (order[:, None] > order[None, :])
     rank = jnp.sum(matches.astype(jnp.int32), axis=2)
     chosen_here = jnp.where(jnp.arange(8) < 4, z, 4 + y)
-    hit = (rank[:, :, None] == jnp.arange(cap)) & (key == chosen_here[:, None])[:, :, None]
-    table = jnp.sum(jnp.where(hit, number[:, :, None], 0), axis=1)
-    used = jnp.sum(hit.astype(jnp.int32), axis=1).reshape(-1)
-    target = (table + jnp.where(jnp.arange(8) < 4, 0, 4 * past.shape[0])[:, None]).reshape(-1)
-    mine = key[z] * cap + rank[z]
     live = grid(kept)[y, x, z]
-
-    arrived = spread(past, table.reshape(-1))
     w_pair = jnp.concatenate([w_key, w_value], axis=1)
-    attn, token_grad, far_grad, seen, dkv, dq, mixed = layer(
-        mine, live, arrived, tokens, grads, w_query, w_pair, w_out, 8 * cap
+    flat = lambda a: a.reshape(-1, a.shape[-1])
+
+    def exchange(cap, ident):
+        hit = (rank[:, :, None] == jnp.arange(cap)) & (key == chosen_here[:, None])[:, :, None]
+        table = jnp.sum(jnp.where(hit, number[:, :, None], 0), axis=1)
+        used = jnp.sum(hit.astype(jnp.int32), axis=1).reshape(-1)
+        target = (table + jnp.where(jnp.arange(8) < 4, 0, 4 * blocks)[:, None]).reshape(-1)
+        mine = jnp.where(live > 0, key[z] * cap + rank[z], 0)
+        arrived = spread(past, table.reshape(-1), ident)
+        attn, token_grad, far_grad, seen, dkv, dq, mixed = layer(
+            mine, live, arrived, tokens, grads, w_query, w_pair, w_out, 8 * cap
+        )
+        returned, *weight_grads = send_back(
+            far_grad, flat(tokens), flat(grads), flat(seen), flat(dkv), flat(dq), flat(mixed), ident + 1
+        )
+        partial = scatter_sum(returned, target, used, 8 * blocks)
+        return attn, token_grad, partial, tuple(weight_grads)
+
+    attn, token_grad, partial, weight_grads = lax.cond(
+        most <= 6, lambda: exchange(6, 0), lambda: exchange(8, 3)
     )
-    flat = lambda a: a.reshape(-1, a.shape[-1])
-    returned, *weight_grads = send_back(
-        far_grad, flat(tokens), flat(grads), flat(seen), flat(dkv), flat(dq), flat(mixed)
-    )
-    partial = scatter_sum(returned, target, used, 8 * past.shape[0])
     scale = 1.0 / math.sqrt(lax.axis_size("dp") * peers * patches * block)
     past_grad, weights = collect(partial.reshape((8,) + past.shape), weight_grads, scale)
     weights = weights.astype(F32)

time: 452 us -> 404 us (0.89)
  Pallas kernels: 435 us -> 386 us
    pallas_call x1, Pallas kernels: 81.4 us -> 59.1 us  [send_back(): pl.pallas_call(kernel, out_shape=(jax.ShapeDtypeStruct(grads.shape, grads...]
    pallas_call x1, Pallas kernels: 139 us -> 122 us  [spread(): pl.pallas_call(kernel, out_shape=jax.ShapeDtypeStruct((8 * cap, rows, wid...]
    pallas_call x1, Pallas kernels: 129 us -> 121 us  [collect(): pl.pallas_call(kernel, out_shape=(jax.ShapeDtypeStruct((blocks, rows, wid...]
where the time goes in v6:
time: 404 us
  Pallas kernels  386 us (96%)
  local copies, waits for them, and re-layouts  11.6 us (3%)
  other arithmetic  4.55 us (1%)
    pallas_call x1, Pallas kernels, spread(): pl.pallas_call(kernel, out_shape=jax.ShapeDtypeStruct((8 * cap, rows, wid...  122 us
    pallas_call x1, Pallas kernels, collect(): pl.pallas_call(kernel, out_shape=(jax.ShapeDtypeStruct((blocks, rows, wid...  121 us
    pallas_call x1, Pallas kernels, layer(): pl.pallas_call(kernel, out_shape=(shape(patches, block, width), shape(pat...  69.8 us
    pallas_call x1, Pallas kernels, send_back(): pl.pallas_call(kernel, out_shape=(jax.ShapeDtypeStruct(grads.shape, grads...  59.1 us
    pallas_call x1, Pallas kernels, scatter_sum(): pl.pallas_call(kernel, out_shape=jax.ShapeDtypeStruct((outputs, rows, wid...  13.5 us

profile of v6, /device:TPU:1, one launch (start us, length us, event | category | flops | bytes accessed | tf_op | source)
XLA Modules:
  0.0 403.6 jit_solution(227882359791620468)
XLA Ops:
  0.7 0.7 broadcast_compare_fusion.4
  1.4 0.1 copy.27
  1.6 0.1 gt.39
  1.7 0.8 copy.28
  2.5 0.1 reshape.213
  2.6 0.1 reshape.211
  2.9 0.6 reduce_max.9
  4.2 0.8 copy.32
  5.0 0.1 reshape.214
  5.2 0.8 copy.30
  6.0 0.1 reshape.212
  6.1 0.1 multiply_add_fusion
  6.3 0.1 and_convert_fusion
  6.4 1.9 pad_maximum_fusion
  8.3 266.2 %conditional.1 = (bf16[2,128,768]{2,1,0:T(8,128)(2,1)}, bf16[2,128,768]{2,1,0:T(8,128)(2,1)}, f32[768,768]{1,0:T(8,128)}, f32[768,768]{1,0:T(8,128)}, f32[768,76...) conditional(s32[]{:T(128)} %convert_element_type.22, (s32[4,2,4,24]{3,2,1,0:T(4,128)S(1)}, ...), branch_computations={%region_2.6_spmd, %region_6.10_spmd} | conditional | flops 13891 | bytes 25718 | solution.py:859
  8.5 0.1 broadcast_compare_fusion.1
  8.6 0.1 add.116
  8.7 0.1 add.117
  8.7 0.2 reduce_sum.63
  9.0 0.5 compare_select_fusion.5
  9.5 0.3 convert_reduce_fusion.1
  9.8 0.1 copy.26
  9.8 0.1 reshape.205.used_ref
  9.9 0.1 copy.25
  10.0 0.1 reshape.200.table_ref
  10.1 122.0 %spread.3.arrived_ref = bf16[48,128,768]{2,1,0:T(8,128)(2,1)} custom-call(s32[48]{0:T(128)S(1)} %reshape.200.table_ref, bf16[8,128,768]{2,1,0:T(8,128)(2,1)} %bitcast.46), custom_call_target="tpu_custom_call" | custom-call | tf_op jit(solution)/shard_map/cond/branch_1_fun/spread/pallas_call | solution.py:167
  132.1 69.8 %layer.5 = (bf16[2,128,768]{2,1,0:T(8,128)(2,1)}, bf16[2,128,768]{2,1,0:T(8,128)(2,1)}, bf16[48,128,768]{2,1,0:T(8,128)(2,1)}, bf16[2,1664,768]{2,1,0:T(8,128)(2...) custom-call(s32[24]{0:T(128)} %get-tuple-element.266.position_ref, ...), custom_call_target="tpu_custom_call" | custom-call | tf_op jit(solution)/shard_map/cond/branch_1_fun/layer/pallas_call | solution.py:774
  201.9 59.1 %send_back.5 = (bf16[48,128,768]{2,1,0:T(8,128)(2,1)}, f32[768,768]{1,0:T(8,128)}, f32[768,768]{1,0:T(8,128)}, f32[768,768]{1,0:T(8,128)}, f32[768,768]{1,0:T(8,128)}) custom-call(bf16[48,128,768]{2,1,0:T(8,128)(2,1)} %get-tuple-element.225.grad_ref, bf16[256,768]{1,0:T(8,128)(2,1)S(1)} %bitcast.50, bf16[256,768]{1,0:T(8,128)(2,1)S(1)} %bitcast.54, ...), custom_call_target="tpu_custom_call" | custom-call | tf_op jit(solution)/shard_map/cond/branch_1_fun/send_back/pallas_call | solution.py:264
  261.0 13.5 %scatter_sum.5 = bf16[64,128,768]{2,1,0:T(8,128)(2,1)} custom-call(s32[48]{0:T(128)S(1)} %add.118.target_ref, s32[48]{0:T(128)S(1)} %reshape.205.used_ref, bf16[48,128,768]{2,1,0:T(8,128)(2,1)} %get-tuple-element.234.source_ref), custom_call_target="tpu_custom_call" | custom-call | tf_op jit(solution)/shard_map/cond/branch_1_fun/scatter_sum/pallas_call | solution.py:626
  274.5 121.3 %collect.1 = (bf16[8,128,768]{2,1,0:T(8,128)(2,1)}, bf16[96,32,768]{2,1,0:T(8,128)(2,1)}) custom-call(bf16[8,8,128,768]{3,2,1,0:T(8,128)(2,1)} %get-tuple-element.253.part_in, f32[768,768]{1,0:T(8,128)} %get-tuple-element.254.a, f32[768,768]{1,0:T(8,128)} %get-tuple-element.255.b, f32[768,768]{1,0:T(8,128)} %get-tuple-element.256.c, ...), custom_call_target="tpu_custom_call" | custom-call | tf_op jit(solution)/shard_map/collect/pallas_call | solution.py:579
  395.8 6.6 %fusion.21 = (f32[24,32,768]{2,1,0:T(8,128)}, f32[24,32,768]{2,1,0:T(8,128)}, f32[24,32,768]{2,1,0:T(8,128)}, f32[24,32,768]{2,1,0:T(8,128)}) fusion(bf16[96,32,768]{2,1,0:T(8,128)(2,1)} %get-tuple-element.259), kind=kLoop, calls=%fused_computation.79 | loop fusion | bytes 18874368 | tf_op jit(solution)/shard_map/slice | solution.py:872
  402.5 1.1 copy.48
  (18 shorter events, 0.2 us)
Async XLA Ops:
  6.4 1.9 copy-start
  6.4 1.9 copy-start.1
  395.8 6.6 %copy-start.2 = (bf16[8,128,768]{2,1,0:T(8,128)(2,1)S(1)}, bf16[8,128,768]{2,1,0:T(8,128)(2,1)}, u32[]{:S(2)}) copy-start(bf16[8,128,768]{2,1,0:T(8,128)(2,1)} %get-tuple-element.258) | copy-start | bytes 4718596
